TPU v7x, 256 devices: a whole 4x4x8 slice. The times are simulated.
256 devices in a mesh: section: 8 (over z), expert: 32 (over y, x, core).
Axes of the slice: x: 4, y: 4, z: 8, core: 2. Of those that a mesh axis runs over, the one named last changes fastest.
Arguments:
- forward_in: bfloat16 [8, 512, 7168], P('section', 'expert'), may hold values from -6 to 6
- reverse_in: bfloat16 [8, 512, 7168], P('section', 'expert'), may hold values from -6 to 6
- norm_gain: bfloat16 [8, 7168], P('section'), may hold values from 0.099609375 to 1.8984375
- gate_up_weight: bfloat16 [8, 2, 7168, 8192], P('section', None, None, 'expert'), may hold values from -0.0625 to 0.0625
- down_weight: bfloat16 [8, 8192, 7168], P('section', 'expert'), may hold values from -0.125 to 0.125
- expert_ids: int32 [8, 2, 2, 512, 1], P('section', None, None, 'expert'), may hold values from 0 to 3; in each aligned block of 16 rows (0 to 15, 16 to 31, ..., all dimensions but the last counted through in order) at most 6 rows name the same one
- gate_weights: float32 [8, 2, 2, 512, 1], P('section', None, None, 'expert'), may hold values from 0.2 to 1
Outputs:
- forward_out: bfloat16 [8, 512, 7168], P('section', 'expert')
- reverse_out: bfloat16 [8, 512, 7168], P('section', 'expert')
Inputs may be any that keep to these rules, and one draw needn't show every extreme that they name: `expert_ids`: in every layer, step and direction, the 16 tokens of one device name any one expert at most 6 times, and in some of these blocks one expert is named exactly 6 times. Each token names exactly one expert.
All inputs are finite; a program needn't handle non-finite values.
Results may differ from a plain program's by a relative error of at most 0.0075.
Values may be sent and summed in bfloat16 or wider, within the bound.
A program may use at most 128 MiB of HBM per device.

v0:
```python
import jax
import jax.numpy as jnp
from jax import lax
from jax.sharding import PartitionSpec as P

EXPERTS = 4
TICKS = 2
MOST = 6


def passed_along(block, axis, distance):
    devices = range(lax.axis_size(axis))
    route = [((i - distance) % len(devices), i) for i in devices]
    return lax.ppermute(block, axis, route)


def expert_share(received, weight_in, weight_out):
    sources, slots, width = received.shape
    flat_rows = received.reshape(sources * slots, width)
    projected = jnp.einsum("rd,kdu->kru", flat_rows, weight_in, preferred_element_type=jnp.float32)
    hidden = (jax.nn.silu(projected[0]) * projected[1]).astype(jnp.bfloat16)
    partial_out = jnp.dot(hidden, weight_out, preferred_element_type=jnp.float32).astype(
        jnp.bfloat16
    )
    return partial_out.reshape(sources, slots, width)


def pass_layer(rows_in, gain, weight_in, weight_out, routes, shares, capacity):
    count, width = rows_in.shape
    top_count = routes.shape[1]
    rows_float = rows_in.astype(jnp.float32)
    scale = lax.rsqrt(jnp.mean(rows_float * rows_float, axis=-1, keepdims=True) + 1e-06)
    normed = (rows_float * scale * gain.astype(jnp.float32)).astype(jnp.bfloat16)
    flat_ids = routes.reshape(-1)
    one_hot = (flat_ids[:, None] == jnp.arange(EXPERTS, dtype=jnp.int32)[None, :]).astype(jnp.int32)
    ranks = jnp.cumsum(one_hot, axis=0) - one_hot
    slot_index = jnp.sum(ranks * one_hot, axis=1)
    target = (flat_ids * capacity + slot_index).reshape(count, top_count)
    places = jnp.arange(EXPERTS * capacity, dtype=jnp.int32)
    picker = jnp.sum(
        (places[:, None, None] == target[None, :, :]).astype(jnp.float32), axis=2
    ).astype(jnp.bfloat16)
    packed = jnp.dot(picker, normed, preferred_element_type=jnp.float32).astype(jnp.bfloat16)
    group = lax.axis_size("expert") // EXPERTS
    outgoing = jnp.repeat(packed.reshape(EXPERTS, capacity, width), group, axis=0)
    partial_out = expert_share(
        lax.all_to_all(outgoing, "expert", split_axis=0, concat_axis=0, tiled=True),
        weight_in,
        weight_out,
    )
    returned = lax.all_to_all(partial_out, "expert", split_axis=0, concat_axis=0, tiled=True)
    summed = jnp.sum(returned.reshape(EXPERTS, group, capacity, width).astype(jnp.float32), axis=1)
    summed = summed.reshape(EXPERTS * capacity, width)
    mixing = jnp.sum(
        jnp.where(
            places[None, None, :] == target[:, :, None],
            shares[:, :, None],
            jnp.zeros_like(shares)[:, :, None],
        ),
        axis=1,
    )
    mixed = rows_float + jnp.dot(
        mixing, summed, precision=lax.Precision.HIGHEST, preferred_element_type=jnp.float32
    )
    return mixed.astype(jnp.bfloat16)


def local(forward_in, reverse_in, norm_gain, gate_up_weight, down_weight, expert_ids, gate_weights):
    forward = forward_in[0]
    reverse = reverse_in[0]
    gain = norm_gain[0]
    weight_in = gate_up_weight[0]
    weight_out = down_weight[0]
    for moment in range(TICKS):
        new_forward = pass_layer(
            forward,
            gain,
            weight_in,
            weight_out,
            expert_ids[0, moment, 0],
            gate_weights[0, moment, 0],
            MOST,
        )
        new_reverse = pass_layer(
            reverse,
            gain,
            weight_in,
            weight_out,
            expert_ids[0, moment, 1],
            gate_weights[0, moment, 1],
            MOST,
        )
        forward = passed_along(new_forward, "section", 1)
        reverse = passed_along(new_reverse, "section", -1)
    return (forward[None], reverse[None])


def solution(mesh):
    in_specs = (
        P("section", "expert", None),
        P("section", "expert", None),
        P("section", None),
        P("section", None, None, "expert"),
        P("section", "expert", None),
        P("section", None, None, "expert", None),
        P("section", None, None, "expert", None),
    )
    out_specs = (P("section", "expert", None), P("section", "expert", None))
    return jax.shard_map(local, mesh=mesh, in_specs=in_specs, out_specs=out_specs, check_vma=False)
```

profile of v0, /device:TPU:1, one launch (start us, length us, event | category | flops | bytes accessed | tf_op | source)
XLA Modules:
  0.0 450.3 jit_solution(11737352010704995663)
XLA Ops:
  8.4 8.8 %all-to-all-start.4 = ((bf16[32,6,7168]{2,1,0:T(8,128)(2,1)}), bf16[32,6,7168]{2,1,0:T(8,128)(2,1)}, u32[]{:S(2)}, u32[]{:S(2)}) async-start(bf16[32,6,7168]{2,1,0:T(8,128)(2,1)} %bitcast.130), calls=%async_computation.4 | async-start | bytes 7340032 | tf_op jit(solution)/shard_map/all_to_all | solution.py:47
  17.8 44.1 %all-to-all-done.4 = bf16[32,6,7168]{2,1,0:T(8,128)(2,1)} async-done(((bf16[32,6,7168]{2,1,0:T(8,128)(2,1)}), bf16[32,6,7168]{2,1,0:T(8,128)(2,1)}, u32[]{:S(2)}, u32[]{:S(2)}) %all-to-all-start.4) | async-done | bytes 2752544 | tf_op jit(solution)/shard_map/all_to_all | solution.py:47
  64.3 7.6 %all-to-all-start = ((bf16[32,6,7168]{2,1,0:T(8,128)(2,1)}), bf16[32,6,7168]{2,1,0:T(8,128)(2,1)}, u32[]{:S(2)}, u32[]{:S(2)}) async-start(bf16[32,6,7168]{2,1,0:T(8,128)(2,1)} %bitcast.128), calls=%async_computation | async-start | bytes 7340032 | tf_op jit(solution)/shard_map/all_to_all | solution.py:47
  71.9 3.2 reshape.646
  75.1 4.8 %fusion.22 = f32[2,192,256]{2,1,0:T(8,128)S(1)} fusion(bf16[192,7168,1]{1,0,2:T(8,128)(2,1)S(1)} %reshape.646, bf16[1,2,7168,256]{3,2,1,0:T(8,128)(2,1)} %param.10), kind=kOutput, calls=%fused_computation.34 | convolution fusion | flops 1409286144 | bytes 10485760 | tf_op jit(solution)/shard_map/rd,kdu->kru/dot_general | solution.py:20
  83.7 33.4 %all-to-all-done = bf16[32,6,7168]{2,1,0:T(8,128)(2,1)} async-done(((bf16[32,6,7168]{2,1,0:T(8,128)(2,1)}), bf16[32,6,7168]{2,1,0:T(8,128)(2,1)}, u32[]{:S(2)}, u32[]{:S(2)}) %all-to-all-start) | async-done | bytes 2752544 | tf_op jit(solution)/shard_map/all_to_all | solution.py:47
  117.1 7.3 %all-to-all-start.5 = ((bf16[32,6,7168]{2,1,0:T(8,128)(2,1)}), bf16[32,6,7168]{2,1,0:T(8,128)(2,1)}, u32[]{:S(2)}, u32[]{:S(2)}) async-start(bf16[32,6,7168]{2,1,0:T(8,128)(2,1)} %reshape.630), calls=%async_computation.5 | async-start | bytes 7340032 | tf_op jit(solution)/shard_map/all_to_all | solution.py:51
  124.4 3.2 reshape.644
  127.6 4.8 %fusion.16 = f32[2,192,256]{2,1,0:T(8,128)S(1)} fusion(bf16[192,7168,1]{1,0,2:T(8,128)(2,1)S(1)} %reshape.644, bf16[1,2,7168,256]{3,2,1,0:T(8,128)(2,1)} %param.10), kind=kOutput, calls=%fused_computation.32 | convolution fusion | flops 1409286144 | bytes 10485760 | tf_op jit(solution)/shard_map/rd,kdu->kru/dot_general | solution.py:20
  136.1 33.5 %all-to-all-done.5 = bf16[32,6,7168]{2,1,0:T(8,128)(2,1)} async-done(((bf16[32,6,7168]{2,1,0:T(8,128)(2,1)}), bf16[32,6,7168]{2,1,0:T(8,128)(2,1)}, u32[]{:S(2)}, u32[]{:S(2)}) %all-to-all-start.5) | async-done | bytes 2752544 | tf_op jit(solution)/shard_map/all_to_all | solution.py:51
  169.6 7.3 %all-to-all-start.1 = ((bf16[32,6,7168]{2,1,0:T(8,128)(2,1)}), bf16[32,6,7168]{2,1,0:T(8,128)(2,1)}, u32[]{:S(2)}, u32[]{:S(2)}) async-start(bf16[32,6,7168]{2,1,0:T(8,128)(2,1)} %reshape.620), calls=%async_computation.1 | async-start | bytes 7340032 | tf_op jit(solution)/shard_map/all_to_all | solution.py:51
  177.0 2.9 convert_reduce_fusion.1
  180.6 5.8 %collective-permute-start.2 = (bf16[16,7168]{1,0:T(8,128)(2,1)S(1)}, bf16[16,7168]{1,0:T(8,128)(2,1)S(1)}, u32[]{:S(2)}, u32[]{:S(2)}) collective-permute-start(bf16[16,7168]{1,0:T(8,128)(2,1)S(1)} %fusion.2), channel_id=1, source_target_pairs={{32,0},{64,32},{96,64},{128,96},{160,128},{192,160},{224,192},{0,2... | collective-permute-start | bytes 688136 | tf_op jit(solution)/shard_map/ppermute | solution.py:14
  186.4 4.6 %collective-permute-done.2 = bf16[16,7168]{1,0:T(8,128)(2,1)S(1)} collective-permute-done((bf16[16,7168]{1,0:T(8,128)(2,1)S(1)}, bf16[16,7168]{1,0:T(8,128)(2,1)S(1)}, u32[]{:S(2)}, u32[]{:S(2)}) %collective-permute-start.2) | collective-permute-done | bytes 229408 | tf_op jit(solution)/shard_map/ppermute | solution.py:14
  191.6 30.5 %all-to-all-done.1 = bf16[32,6,7168]{2,1,0:T(8,128)(2,1)} async-done(((bf16[32,6,7168]{2,1,0:T(8,128)(2,1)}), bf16[32,6,7168]{2,1,0:T(8,128)(2,1)}, u32[]{:S(2)}, u32[]{:S(2)}) %all-to-all-start.1) | async-done | bytes 2752544 | tf_op jit(solution)/shard_map/all_to_all | solution.py:51
  224.5 7.2 %all-to-all-start.6 = ((bf16[32,6,7168]{2,1,0:T(8,128)(2,1)}), bf16[32,6,7168]{2,1,0:T(8,128)(2,1)}, u32[]{:S(2)}, u32[]{:S(2)}) async-start(bf16[32,6,7168]{2,1,0:T(8,128)(2,1)} %bitcast.127), calls=%async_computation.6 | async-start | bytes 7340032 | tf_op jit(solution)/shard_map/all_to_all | solution.py:47
  231.8 2.9 convert_reduce_fusion.3
  237.1 9.7 %collective-permute-done = bf16[16,7168]{1,0:T(8,128)(2,1)S(1)} collective-permute-done((bf16[16,7168]{1,0:T(8,128)(2,1)S(1)}, bf16[16,7168]{1,0:T(8,128)(2,1)S(1)}, u32[]{:S(2)}, u32[]{:S(2)}) %collective-permute-start) | collective-permute-done | bytes 229408 | tf_op jit(solution)/shard_map/ppermute | solution.py:14
  247.4 29.6 %all-to-all-done.6 = bf16[32,6,7168]{2,1,0:T(8,128)(2,1)} async-done(((bf16[32,6,7168]{2,1,0:T(8,128)(2,1)}), bf16[32,6,7168]{2,1,0:T(8,128)(2,1)}, u32[]{:S(2)}, u32[]{:S(2)}) %all-to-all-start.6) | async-done | bytes 2752544 | tf_op jit(solution)/shard_map/all_to_all | solution.py:47
  279.3 7.3 %all-to-all-start.2 = ((bf16[32,6,7168]{2,1,0:T(8,128)(2,1)}), bf16[32,6,7168]{2,1,0:T(8,128)(2,1)}, u32[]{:S(2)}, u32[]{:S(2)}) async-start(bf16[32,6,7168]{2,1,0:T(8,128)(2,1)} %bitcast.129), calls=%async_computation.2 | async-start | bytes 7340032 | tf_op jit(solution)/shard_map/all_to_all | solution.py:47
  286.5 3.2 reshape.647
  289.8 4.8 %fusion.25 = f32[2,192,256]{2,1,0:T(8,128)S(1)} fusion(bf16[192,7168,1]{1,0,2:T(8,128)(2,1)S(1)} %reshape.647, bf16[1,2,7168,256]{3,2,1,0:T(8,128)(2,1)} %param.10), kind=kOutput, calls=%fused_computation.35 | convolution fusion | flops 1409286144 | bytes 10485760 | tf_op jit(solution)/shard_map/rd,kdu->kru/dot_general | solution.py:20
  298.3 33.5 %all-to-all-done.2 = bf16[32,6,7168]{2,1,0:T(8,128)(2,1)} async-done(((bf16[32,6,7168]{2,1,0:T(8,128)(2,1)}), bf16[32,6,7168]{2,1,0:T(8,128)(2,1)}, u32[]{:S(2)}, u32[]{:S(2)}) %all-to-all-start.2) | async-done | bytes 2752544 | tf_op jit(solution)/shard_map/all_to_all | solution.py:47
  331.8 7.2 %all-to-all-start.7 = ((bf16[32,6,7168]{2,1,0:T(8,128)(2,1)}), bf16[32,6,7168]{2,1,0:T(8,128)(2,1)}, u32[]{:S(2)}, u32[]{:S(2)}) async-start(bf16[32,6,7168]{2,1,0:T(8,128)(2,1)} %reshape.635), calls=%async_computation.7 | async-start | bytes 7340032 | tf_op jit(solution)/shard_map/all_to_all | solution.py:51
  339.1 3.2 reshape.645
  342.3 4.8 %fusion.19 = f32[2,192,256]{2,1,0:T(8,128)S(1)} fusion(bf16[192,7168,1]{1,0,2:T(8,128)(2,1)S(1)} %reshape.645, bf16[1,2,7168,256]{3,2,1,0:T(8,128)(2,1)} %param.10), kind=kOutput, calls=%fused_computation.33 | convolution fusion | flops 1409286144 | bytes 10485760 | tf_op jit(solution)/shard_map/rd,kdu->kru/dot_general | solution.py:20
  350.8 33.5 %all-to-all-done.7 = bf16[32,6,7168]{2,1,0:T(8,128)(2,1)} async-done(((bf16[32,6,7168]{2,1,0:T(8,128)(2,1)}), bf16[32,6,7168]{2,1,0:T(8,128)(2,1)}, u32[]{:S(2)}, u32[]{:S(2)}) %all-to-all-start.7) | async-done | bytes 2752544 | tf_op jit(solution)/shard_map/all_to_all | solution.py:51
  384.3 7.3 %all-to-all-start.3 = ((bf16[32,6,7168]{2,1,0:T(8,128)(2,1)}), bf16[32,6,7168]{2,1,0:T(8,128)(2,1)}, u32[]{:S(2)}, u32[]{:S(2)}) async-start(bf16[32,6,7168]{2,1,0:T(8,128)(2,1)} %reshape.625), calls=%async_computation.3 | async-start | bytes 7340032 | tf_op jit(solution)/shard_map/all_to_all | solution.py:51
  391.8 2.9 convert_reduce_fusion
  395.3 5.7 %collective-permute-start.3 = (bf16[16,7168]{1,0:T(8,128)(2,1)S(1)}, bf16[16,7168]{1,0:T(8,128)(2,1)S(1)}, u32[]{:S(2)}, u32[]{:S(2)}) collective-permute-start(bf16[16,7168]{1,0:T(8,128)(2,1)S(1)} %fusion.3), channel_id=1, source_target_pairs={{32,0},{64,32},{96,64},{128,96},{160,128},{192,160},{224,192},{0,2... | collective-permute-start | bytes 688136 | tf_op jit(solution)/shard_map/ppermute | solution.py:14
  401.0 35.3 %all-to-all-done.3 = bf16[32,6,7168]{2,1,0:T(8,128)(2,1)} async-done(((bf16[32,6,7168]{2,1,0:T(8,128)(2,1)}), bf16[32,6,7168]{2,1,0:T(8,128)(2,1)}, u32[]{:S(2)}, u32[]{:S(2)}) %all-to-all-start.3) | async-done | bytes 2752544 | tf_op jit(solution)/shard_map/all_to_all | solution.py:51
  441.6 7.3 %collective-permute-done.1 = bf16[16,7168]{1,0:T(8,128)(2,1)S(1)} collective-permute-done((bf16[16,7168]{1,0:T(8,128)(2,1)S(1)}, bf16[16,7168]{1,0:T(8,128)(2,1)S(1)}, u32[]{:S(2)}, u32[]{:S(2)}) %collective-permute-start.1) | collective-permute-done | bytes 229408 | tf_op jit(solution)/shard_map/ppermute | solution.py:14
  (74 shorter events, 41.9 us)
Async XLA Ops:
  8.4 8.8 %copy-start.5 = (bf16[1,16,7168]{2,1,0:T(8,128)(2,1)S(1)}, bf16[1,16,7168]{2,1,0:T(8,128)(2,1)}, u32[]{:S(2)}) copy-start(bf16[1,16,7168]{2,1,0:T(8,128)(2,1)} %param.7) | copy-start | bytes 688132
  8.4 53.6 %all-to-all-start.4 = ((bf16[32,6,7168]{2,1,0:T(8,128)(2,1)}), bf16[32,6,7168]{2,1,0:T(8,128)(2,1)}, u32[]{:S(2)}, u32[]{:S(2)}) async-start(bf16[32,6,7168]{2,1,0:T(8,128)(2,1)} %bitcast.130), calls=%async_computation.4 | async-start | bytes 7340032 | tf_op jit(solution)/shard_map/all_to_all | solution.py:47
  64.3 52.8 %all-to-all-start = ((bf16[32,6,7168]{2,1,0:T(8,128)(2,1)}), bf16[32,6,7168]{2,1,0:T(8,128)(2,1)}, u32[]{:S(2)}, u32[]{:S(2)}) async-start(bf16[32,6,7168]{2,1,0:T(8,128)(2,1)} %bitcast.128), calls=%async_computation | async-start | bytes 7340032 | tf_op jit(solution)/shard_map/all_to_all | solution.py:47
  75.1 4.8 %copy-start = (bf16[1,256,7168]{2,1,0:T(8,128)(2,1)S(1)}, bf16[1,256,7168]{2,1,0:T(8,128)(2,1)}, u32[]{:S(2)}) copy-start(bf16[1,256,7168]{2,1,0:T(8,128)(2,1)} %param.11) | copy-start | bytes 11010052
  117.1 52.5 %all-to-all-start.5 = ((bf16[32,6,7168]{2,1,0:T(8,128)(2,1)}), bf16[32,6,7168]{2,1,0:T(8,128)(2,1)}, u32[]{:S(2)}, u32[]{:S(2)}) async-start(bf16[32,6,7168]{2,1,0:T(8,128)(2,1)} %reshape.630), calls=%async_computation.5 | async-start | bytes 7340032 | tf_op jit(solution)/shard_map/all_to_all | solution.py:51
  127.6 4.8 %copy-start.1 = (bf16[1,256,7168]{2,1,0:T(8,128)(2,1)S(1)}, bf16[1,256,7168]{2,1,0:T(8,128)(2,1)}, u32[]{:S(2)}) copy-start(bf16[1,256,7168]{2,1,0:T(8,128)(2,1)} %param.11) | copy-start | bytes 11010052
  136.1 40.8 %copy-start.6 = (f32[1,2,2,16,1]{3,4,2,1,0:T(1,128)S(1)}, f32[1,2,2,16,1]{3,4,2,1,0:T(1,128)}, u32[]{:S(2)}) copy-start(f32[1,2,2,16,1]{3,4,2,1,0:T(1,128)} %param.13) | copy-start | bytes 772
  169.6 52.5 %all-to-all-start.1 = ((bf16[32,6,7168]{2,1,0:T(8,128)(2,1)}), bf16[32,6,7168]{2,1,0:T(8,128)(2,1)}, u32[]{:S(2)}, u32[]{:S(2)}) async-start(bf16[32,6,7168]{2,1,0:T(8,128)(2,1)} %reshape.620), calls=%async_computation.1 | async-start | bytes 7340032 | tf_op jit(solution)/shard_map/all_to_all | solution.py:51
  176.9 3.1 copy-start.4
  180.6 10.4 %collective-permute-start.2 = (bf16[16,7168]{1,0:T(8,128)(2,1)S(1)}, bf16[16,7168]{1,0:T(8,128)(2,1)S(1)}, u32[]{:S(2)}, u32[]{:S(2)}) collective-permute-start(bf16[16,7168]{1,0:T(8,128)(2,1)S(1)} %fusion.2), channel_id=1, source_target_pairs={{32,0},{64,32},{96,64},{128,96},{160,128},{192,160},{224,192},{0,2... | collective-permute-start | bytes 688136 | tf_op jit(solution)/shard_map/ppermute | solution.py:14
  224.5 52.5 %all-to-all-start.6 = ((bf16[32,6,7168]{2,1,0:T(8,128)(2,1)}), bf16[32,6,7168]{2,1,0:T(8,128)(2,1)}, u32[]{:S(2)}, u32[]{:S(2)}) async-start(bf16[32,6,7168]{2,1,0:T(8,128)(2,1)} %bitcast.127), calls=%async_computation.6 | async-start | bytes 7340032 | tf_op jit(solution)/shard_map/all_to_all | solution.py:47
  235.4 11.4 %collective-permute-start = (bf16[16,7168]{1,0:T(8,128)(2,1)S(1)}, bf16[16,7168]{1,0:T(8,128)(2,1)S(1)}, u32[]{:S(2)}, u32[]{:S(2)}) collective-permute-start(bf16[16,7168]{1,0:T(8,128)(2,1)S(1)} %fusion), channel_id=1, source_target_pairs={{224,0},{0,32},{32,64},{64,96},{96,128},{128,160},{160,192},{192,2... | collective-permute-start | bytes 688136 | tf_op jit(solution)/shard_map/ppermute | solution.py:14
  279.3 52.5 %all-to-all-start.2 = ((bf16[32,6,7168]{2,1,0:T(8,128)(2,1)}), bf16[32,6,7168]{2,1,0:T(8,128)(2,1)}, u32[]{:S(2)}, u32[]{:S(2)}) async-start(bf16[32,6,7168]{2,1,0:T(8,128)(2,1)} %bitcast.129), calls=%async_computation.2 | async-start | bytes 7340032 | tf_op jit(solution)/shard_map/all_to_all | solution.py:47
  289.8 4.8 %copy-start.2 = (bf16[1,256,7168]{2,1,0:T(8,128)(2,1)S(1)}, bf16[1,256,7168]{2,1,0:T(8,128)(2,1)}, u32[]{:S(2)}) copy-start(bf16[1,256,7168]{2,1,0:T(8,128)(2,1)} %param.11) | copy-start | bytes 11010052
  331.8 52.5 %all-to-all-start.7 = ((bf16[32,6,7168]{2,1,0:T(8,128)(2,1)}), bf16[32,6,7168]{2,1,0:T(8,128)(2,1)}, u32[]{:S(2)}, u32[]{:S(2)}) async-start(bf16[32,6,7168]{2,1,0:T(8,128)(2,1)} %reshape.635), calls=%async_computation.7 | async-start | bytes 7340032 | tf_op jit(solution)/shard_map/all_to_all | solution.py:51
  342.3 4.8 %copy-start.3 = (bf16[1,256,7168]{2,1,0:T(8,128)(2,1)S(1)}, bf16[1,256,7168]{2,1,0:T(8,128)(2,1)}, u32[]{:S(2)}) copy-start(bf16[1,256,7168]{2,1,0:T(8,128)(2,1)} %param.11) | copy-start | bytes 11010052
  384.3 52.0 %all-to-all-start.3 = ((bf16[32,6,7168]{2,1,0:T(8,128)(2,1)}), bf16[32,6,7168]{2,1,0:T(8,128)(2,1)}, u32[]{:S(2)}, u32[]{:S(2)}) async-start(bf16[32,6,7168]{2,1,0:T(8,128)(2,1)} %reshape.625), calls=%async_computation.3 | async-start | bytes 7340032 | tf_op jit(solution)/shard_map/all_to_all | solution.py:51
  395.3 46.2 %collective-permute-start.3 = (bf16[16,7168]{1,0:T(8,128)(2,1)S(1)}, bf16[16,7168]{1,0:T(8,128)(2,1)S(1)}, u32[]{:S(2)}, u32[]{:S(2)}) collective-permute-start(bf16[16,7168]{1,0:T(8,128)(2,1)S(1)} %fusion.3), channel_id=1, source_target_pairs={{32,0},{64,32},{96,64},{128,96},{160,128},{192,160},{224,192},{0,2... | collective-permute-start | bytes 688136 | tf_op jit(solution)/shard_map/ppermute | solution.py:14
  439.9 9.1 %collective-permute-start.1 = (bf16[16,7168]{1,0:T(8,128)(2,1)S(1)}, bf16[16,7168]{1,0:T(8,128)(2,1)S(1)}, u32[]{:S(2)}, u32[]{:S(2)}) collective-permute-start(bf16[16,7168]{1,0:T(8,128)(2,1)S(1)} %fusion.1), channel_id=1, source_target_pairs={{224,0},{0,32},{32,64},{64,96},{96,128},{128,160},{160,192},{192,2... | collective-permute-start | bytes 688136 | tf_op jit(solution)/shard_map/ppermute | solution.py:14
where the time goes:
time: 453 us; the launch traced here: 450 us
  waiting for transfers between devices  295 us (65%)
  starting transfers between devices  74.8 us (17%)
  local copies, waits for them, and re-layouts  36.2 us (8%)
  matrix products  27.2 us (6%)
  other arithmetic  15.9 us (4%)
    all_to_all x4, waiting for transfers between devices, pass_layer(): lax.all_to_all(outgoing, 'expert', split_axis=0, concat_axis=0, tiled=True)  141 us
    all_to_all x4, waiting for transfers between devices, pass_layer(): lax.all_to_all(partial_out, 'expert', split_axis=0, concat_axis=0, tiled=...  133 us
    all_to_all x4, starting transfers between devices, pass_layer(): lax.all_to_all(outgoing, 'expert', split_axis=0, concat_axis=0, tiled=True)  30.9 us
    all_to_all x4, starting transfers between devices, pass_layer(): lax.all_to_all(partial_out, 'expert', split_axis=0, concat_axis=0, tiled=...  29 us
    ppermute x4, waiting for transfers between devices, passed_along(): return lax.ppermute(block, axis, route)  21.6 us
    dot_general x4, matrix products, expert_share(): jnp.einsum('rd,kdu->kru', flat_rows, weight_in, preferred_element_type=jn...  19.3 us
    ppermute x4, starting transfers between devices, passed_along(): return lax.ppermute(block, axis, route)  14.9 us
    reshape x4, local copies, waits for them, and re-layouts, expert_share(): flat_rows = received.reshape(sources * slots, width)  12.9 us
  transfers between devices with their start and end apart: 12, of which 11 were waited for; matrix products, arithmetic and copies ran while one was open for 14% of the time, Pallas kernels for 0%

commit v1 on v0

v1 whole, which is shorter than its diff:
```python
import functools

import jax
import jax.numpy as jnp
from jax import lax
from jax.experimental import pallas as pl
from jax.experimental.pallas import tpu as pltpu
from jax.sharding import PartitionSpec as P

EXPERTS = 4
TICKS = 2
MOST = 6
WIDTH = 7168
HALF = WIDTH // 2
CHUNK = 512
STEPS = HALF // CHUNK
NX = NY = 4
PACK = 4 * MOST
BLOCK = NY * PACK
UNITS = 256
TOK = 16
MESH = pl.DeviceIdType.MESH


def kernel(
    fwd, rev, gain, wgu, wdn, mrow, mcol,
    outf, outr,
    rows, pk, xg, acc, ss, exg, exs, hid, wg, wd,
    rs1s, rs1r, rs2s, rs2r, yrs, yrr, zs, mrow2, mcol2, pick, pickt, mix,
    sem_row, sem_w, sem_m,
    row_s, row_r, w_s, w_r, m_s, m_r,
    yd_s, yd_r, xd_s, xd_r, xr_s, xr_r,
    ex_s, ex_r, hd_s, hd_r,
    r1_s, r1_r, r2_s, r2_r, yr_s, yr_r, z_s, z_r, zf_s, zf_r,
):
    s = lax.axis_index("section")
    me = lax.axis_index("expert")
    ns = lax.axis_size("section")
    c = lax.rem(me, 2)
    o = 1 - c
    x = lax.rem(me // 2, NX)
    y = me // (2 * NX)
    xp, xm, xo = lax.rem(x + 1, NX), lax.rem(x + NX - 1, NX), lax.rem(x + 2, NX)
    sp, sm = lax.rem(s + 1, ns), lax.rem(s + ns - 1, ns)

    def at(yy, xx, cc):
        return (s, (yy * NX + xx) * 2 + cc)

    partner = at(y, x, o)
    right, left = at(y, xp, c), at(y, xm, c)
    ups = [at(lax.rem(y + j, NY), x, c) for j in range(1, NY)]
    zdev = [[(sp, me - c + cc), (sm, me - c + cc)] for cc in range(2)]
    zsame = [(sp, me), (sm, me)]
    zother = [(sp, me - c + o), (sm, me - c + o)]

    def rcopy(src, dst, ssem, rsem, dev):
        return pltpu.make_async_remote_copy(
            src_ref=src, dst_ref=dst, send_sem=ssem, recv_sem=rsem,
            device_id=dev, device_id_type=MESH,
        )

    barrier = pltpu.get_barrier_semaphore()
    peers = [partner, right, left] + ups + zsame + zother
    for dev in peers:
        pl.semaphore_signal(barrier, inc=1, device_id=dev, device_id_type=MESH)
    pl.semaphore_wait(barrier, len(peers))

    def col(half, k):
        return pl.ds(pl.multiple_of(half * HALF + k * CHUNK, CHUNK), CHUNK)

    def row_copies(k):
        both = []
        for d, src in enumerate((fwd, rev)):
            both.append(pltpu.make_async_copy(
                src.at[:, col(c, k)], rows.at[0, k, 2 * d + c], sem_row.at[k, d]))
            both.append(rcopy(
                src.at[:, col(o, k)], rows.at[0, k, 2 * d + c], row_s.at[k, d], row_r.at[k, d], partner))
        return both

    def row_arrivals(k):
        return [
            rcopy(rows.at[0, k, 2 * d + o], rows.at[0, k, 2 * d + o], row_s.at[k, d], row_r.at[k, d], partner)
            for d in range(2)
        ]

    def weight_copies(k):
        made = []
        for g in range(2):
            made.append(pltpu.make_async_copy(
                wgu.at[g, col(c, k), :], wg.at[k, 2 * g + c], sem_w.at[k, g]))
            made.append(rcopy(
                wgu.at[g, col(o, k), :], wg.at[k, 2 * g + c], w_s.at[k, g], w_r.at[k, g], partner))
        made.append(pltpu.make_async_copy(wdn.at[:, col(c, k)], wd.at[k, c], sem_w.at[k, 2]))
        made.append(rcopy(wdn.at[:, col(o, k)], wd.at[k, c], w_s.at[k, 2], w_r.at[k, 2], partner))
        return made

    def weight_arrivals(k):
        return [
            rcopy(wg.at[k, 2 * g + o], wg.at[k, 2 * g + o], w_s.at[k, g], w_r.at[k, g], partner) for g in range(2)
        ] + [rcopy(wd.at[k, o], wd.at[k, o], w_s.at[k, 2], w_r.at[k, 2], partner)]

    tables = [
        rcopy(mrow, mrow2, m_s.at[0], m_r.at[0], partner),
        rcopy(mcol, mcol2, m_s.at[1], m_r.at[1], partner),
    ]
    for t in tables:
        t.start()

    @pl.loop(0, STEPS)
    def _(k):
        for cp in row_copies(k):
            cp.start()

    for t in tables:
        t.wait_recv()
    table_row = mrow[...] + mrow2[...]
    table_col = mcol[...] + mcol2[...]
    for t in range(TICKS):
        slot = lax.broadcasted_iota(jnp.int32, (4 * PACK, 4 * TOK), 0).astype(jnp.float32)
        pick[t] = jnp.where(slot == table_row[t:t + 1, :4 * TOK], 1.0, 0.0).astype(jnp.bfloat16)
        slot_t = lax.broadcasted_iota(jnp.int32, (4 * TOK, 4 * PACK), 1).astype(jnp.float32)
        pickt[t] = jnp.where(slot_t == table_col[:, 2 + t:3 + t], 1.0, 0.0).astype(jnp.bfloat16)
        mix[t] = jnp.broadcast_to(table_col[:, t:t + 1], (4 * TOK, 128))

    def yd(t, k, j):
        e = lax.rem(y + j, NY)
        return rcopy(pk.at[t, k, e], xg.at[t, k, x, y], yd_s.at[t, k, j - 1], yd_r.at[t, k, j - 1], ups[j - 1])

    def yd_in(t, k, j):
        spot = xg.at[t, k, x, lax.rem(y + NY - j, NY)]
        return rcopy(spot, spot, yd_s.at[t, k, j - 1], yd_r.at[t, k, j - 1], ups[j - 1])

    def z_next(t, k, d):
        return rcopy(
            zs.at[t, k, pl.ds(2 * d, 2)], rows.at[1, k, pl.ds(2 * d, 2)], z_s.at[k, d], z_r.at[k, d], zsame[d])

    def d0(t, k):
        if t == 0:
            for cp in row_copies(k):
                if not cp.is_remote:
                    cp.wait()
            for cp in row_arrivals(k):
                cp.wait_recv()
        else:
            for d in range(2):
                z_next(0, k, d).wait_recv()
        chunk = rows[t, k].reshape(4 * TOK, CHUNK)
        packed = jnp.dot(pick[t], chunk, preferred_element_type=jnp.float32)
        pk[t, k] = packed.reshape(NY, PACK, CHUNK).astype(jnp.bfloat16)
        for j in range(1, NY):
            yd(t, k, j).start()
        xg[t, k, x, y] = pk[t, k, y]

    def xd(t, k, way):
        spot = xg.at[t, k, x]
        return rcopy(spot, spot, xd_s.at[t, k, way], xd_r.at[t, k, way], (right, left)[way])

    def xd_in(t, k, way):
        spot = xg.at[t, k, (xm, xp)[way]]
        return rcopy(spot, spot, xd_s.at[t, k, way], xd_r.at[t, k, way], (right, left)[way])

    def d1(t, k):
        for j in range(1, NY):
            yd_in(t, k, j).wait_recv()
        for way in range(2):
            xd(t, k, way).start()

    def xr(t, k, way):
        spot = xg.at[t, k, (xm, xp)[way], pl.ds(2 * way, 2)]
        return rcopy(spot, spot, xr_s.at[t, k, way], xr_r.at[t, k, way], (right, left)[way])

    def xr_in(t, k, way):
        spot = xg.at[t, k, xo, pl.ds(2 * way, 2)]
        return rcopy(spot, spot, xr_s.at[t, k, way], xr_r.at[t, k, way], (right, left)[way])

    def d2(t, k):
        for way in range(2):
            xd_in(t, k, way).wait_recv()
            xr(t, k, way).start()

    def d3(t, k):
        for way in range(2):
            xr_in(t, k, way).wait_recv()
        if t == 0:
            for cp in weight_copies(k):
                if not cp.is_remote:
                    cp.wait()
            for cp in weight_arrivals(k):
                cp.wait_recv()
        held = xg[t, k].reshape(NX * BLOCK, CHUNK).astype(jnp.float32)
        square = held * held
        part = square[:, :128]
        for i in range(1, CHUNK // 128):
            part = part + square[:, 128 * i:128 * (i + 1)]
        scaled = (held * gain[c * STEPS + k]).astype(jnp.bfloat16)

        @pl.when(k == 0)
        def _():
            ss[t] = part.reshape(NX, BLOCK, 128)
            for q in range(4):
                acc[t, q] = jnp.dot(scaled, wg[k, q], preferred_element_type=jnp.float32).reshape(NX, BLOCK, UNITS)

        @pl.when(k > 0)
        def _():
            ss[t] += part.reshape(NX, BLOCK, 128)
            for q in range(4):
                acc[t, q] += jnp.dot(scaled, wg[k, q], preferred_element_type=jnp.float32).reshape(NX, BLOCK, UNITS)

    def ex(t, j):
        return [
            rcopy(acc.at[t, o, j], exg.at[t, 0, j], ex_s.at[t, 0, j], ex_r.at[t, 0, j], partner),
            rcopy(acc.at[t, 2 + o, j], exg.at[t, 1, j], ex_s.at[t, 1, j], ex_r.at[t, 1, j], partner),
            rcopy(ss.at[t, j], exs.at[t, j], ex_s.at[t, 2, j], ex_r.at[t, 2, j], partner),
        ]

    def hd(t, j):
        return rcopy(hid.at[t, c, j], hid.at[t, c, j], hd_s.at[t, j], hd_r.at[t, j], partner)

    def hd_in(t, j):
        return rcopy(hid.at[t, o, j], hid.at[t, o, j], hd_s.at[t, j], hd_r.at[t, j], partner)

    def middle(t):
        @pl.loop(0, NX)
        def _(i):
            for cp in ex(t, lax.rem(x + 2 + i, NX)):
                cp.start()

        @pl.loop(0, NX)
        def _(i):
            j = lax.rem(x + 2 + i, NX)
            for cp in ex(t, j):
                cp.wait_recv()
            total = jnp.sum(ss[t, j] + exs[t, j], axis=-1, keepdims=True)
            scale = lax.rsqrt(total * (1.0 / WIDTH) + 1e-06)
            gate = (acc[t, c, j] + exg[t, 0, j]) * scale
            up = (acc[t, 2 + c, j] + exg[t, 1, j]) * scale
            hid[t, c, j] = (gate / (1.0 + jnp.exp(-gate)) * up).astype(jnp.bfloat16)
            hd(t, j).start()

        @pl.loop(0, NX)
        def _(i):
            hd_in(t, lax.rem(x + 2 + i, NX)).wait_recv()

    def down(t, k, j):
        return jnp.dot(hid[t, 0, j], wd[k, 0], preferred_element_type=jnp.float32) + jnp.dot(
            hid[t, 1, j], wd[k, 1], preferred_element_type=jnp.float32)

    def r1(t, k, way):
        return rcopy(
            rs1s.at[t, k, way], rs1r.at[t, k, way], r1_s.at[t, k, way], r1_r.at[t, k, way], (right, left)[way])

    def r2(t, k, way):
        return rcopy(
            rs2s.at[t, k, way], rs2r.at[t, k, way], r2_s.at[t, k, way], r2_r.at[t, k, way], (right, left)[way])

    def c0(t, k):
        rs1s[t, k] = down(t, k, xo).reshape(2, BLOCK // 2, CHUNK).astype(jnp.bfloat16)
        for way in range(2):
            r1(t, k, way).start()

    def c1(t, k):
        for way in range(2):
            r1(t, k, way).wait_recv()
            part = down(t, k, (xp, xm)[way]).reshape(2, BLOCK // 2, CHUNK)
            got = rs1r[t, k, way].astype(jnp.float32)
            rs2s[t, k, way, way] = (part[way] + got).astype(jnp.bfloat16)
            rs2s[t, k, way, 1 - way] = part[1 - way].astype(jnp.bfloat16)
            r2(t, k, way).start()

    def yr(t, k, j):
        to = lax.rem(y + j, NY)
        return rcopy(yrs.at[t, k, to], yrr.at[t, k, y], yr_s.at[t, k, j - 1], yr_r.at[t, k, j - 1], ups[j - 1])

    def yr_in(t, k, j):
        spot = yrr.at[t, k, lax.rem(y + NY - j, NY)]
        return rcopy(spot, spot, yr_s.at[t, k, j - 1], yr_r.at[t, k, j - 1], ups[j - 1])

    def c2(t, k):
        for way in range(2):
            r2(t, k, way).wait_recv()
        full = down(t, k, x).reshape(2, BLOCK // 2, CHUNK)
        full = full + rs2r[t, k, 0].astype(jnp.float32) + rs2r[t, k, 1].astype(jnp.float32)
        yrs[t, k] = full.reshape(NY, PACK, CHUNK).astype(jnp.bfloat16)
        for j in range(1, NY):
            yr(t, k, j).start()
        yrr[t, k, y] = yrs[t, k, y]

    def z_last(k, d, cc):
        dst = (outf, outr)[d]
        return rcopy(zs.at[1, k, 2 * d + cc], dst.at[:, col(c, k)], zf_s.at[k, d, cc], zf_r.at[k, d, c], zdev[cc][d])

    def z_last_in(k, d, half):
        spot = (outf, outr)[d].at[:, col(half, k)]
        return rcopy(spot, spot, zf_s.at[k, d, half], zf_r.at[k, d, half], zsame[d])

    def c3(t, k):
        for j in range(1, NY):
            yr_in(t, k, j).wait_recv()
        back = yrr[t, k].astype(jnp.float32).reshape(4 * PACK, CHUNK).astype(jnp.bfloat16)
        mine = jnp.dot(pickt[t], back, preferred_element_type=jnp.float32)
        kept = rows[t, k].reshape(4 * TOK, CHUNK).astype(jnp.float32)
        made = kept + mix[t][:, :1] * mine
        zs[t, k] = made.reshape(4, TOK, CHUNK).astype(jnp.bfloat16)
        for d in range(2):
            if t == 0:
                z_next(0, k, d).start()
            else:
                for cc in range(2):
                    z_last(k, d, cc).start()

    def run(stages, steps):
        @pl.loop(0, steps)
        def _(i):
            for lag, f in stages:
                k = i - lag

                @pl.when((k >= 0) & (k < STEPS))
                def _():
                    f(k)

    def start_weights(k):
        for cp in weight_copies(k):
            cp.start()

    dispatch = [d0, d1, d2, d3]
    combine = [c0, c1, c2, c3]
    run([(0, functools.partial(d0, 0)), (0, start_weights), (1, functools.partial(d1, 0)),
         (2, functools.partial(d2, 0)), (3, functools.partial(d3, 0))], STEPS + 3)
    middle(0)
    run([(i, functools.partial(f, 0)) for i, f in enumerate(combine)]
        + [(4 + i, functools.partial(f, 1)) for i, f in enumerate(dispatch)], STEPS + 7)
    middle(1)
    run([(i, functools.partial(f, 1)) for i, f in enumerate(combine)], STEPS + 3)

    for t in tables:
        t.wait_send()

    @pl.loop(0, STEPS)
    def _(k):
        for d in range(2):
            for half in range(2):
                z_last_in(k, d, half).wait_recv()
                z_last(k, d, half).wait_send()
            z_next(0, k, d).wait_send()
        for cp in row_copies(k) + weight_copies(k):
            if cp.is_remote:
                cp.wait_send()
        for t in range(TICKS):
            for j in range(1, NY):
                yd(t, k, j).wait_send()
                yr(t, k, j).wait_send()
            for way in range(2):
                xd(t, k, way).wait_send()
                xr(t, k, way).wait_send()
                r1(t, k, way).wait_send()
                r2(t, k, way).wait_send()

    @pl.loop(0, NX)
    def _(j):
        for t in range(TICKS):
            for cp in ex(t, j):
                cp.wait_send()
            hd(t, j).wait_send()


def local(forward_in, reverse_in, norm_gain, gate_up_weight, down_weight, expert_ids, gate_weights):
    core = lax.rem(lax.axis_index("expert"), 2)
    ids = expert_ids[0, :, :, :, 0]
    earlier = jnp.arange(TOK)[None, :] < jnp.arange(TOK)[:, None]
    rank = jnp.sum((ids[:, :, :, None] == ids[:, :, None, :]) & earlier, axis=-1).astype(jnp.int32)
    way = jnp.arange(2, dtype=jnp.int32)[None, :, None]
    target = (ids * PACK + way * (2 * MOST) + core * MOST + rank).astype(jnp.float32)
    weight = gate_weights[0, :, :, :, 0]
    own = (jnp.arange(2) == core)[None, None, :, None]

    def spread(v):
        return jnp.where(own, v[:, :, None, :], 0.0).reshape(TICKS, 4 * TOK)

    target, weight = spread(target), spread(weight)
    table_row = jnp.pad(target, ((0, 8 - TICKS), (0, 128 - 4 * TOK)))
    table_col = jnp.pad(jnp.concatenate([weight, target], axis=0).T, ((0, 0), (0, 128 - 2 * TICKS)))
    gain = norm_gain[0].astype(jnp.float32).reshape(2 * STEPS, 1, CHUNK)

    bf, f32 = jnp.bfloat16, jnp.float32
    vmem = pltpu.VMEM
    dma = lambda *shape: pltpu.SemaphoreType.DMA(shape)
    anywhere = pl.BlockSpec(memory_space=pl.ANY)
    here = pl.BlockSpec(memory_space=pltpu.VMEM)
    T, K = TICKS, STEPS
    out = jax.ShapeDtypeStruct((TOK, WIDTH), bf)
    outs = pl.pallas_call(
        kernel,
        out_shape=(out, out),
        in_specs=[anywhere, anywhere, here, anywhere, anywhere, here, here],
        out_specs=(here, here),
        scratch_shapes=[
            vmem((T, K, 4, TOK, CHUNK), bf),
            vmem((T, K, NY, PACK, CHUNK), bf),
            vmem((T, K, NX, NY, PACK, CHUNK), bf),
            vmem((T, 4, NX, BLOCK, UNITS), f32),
            vmem((T, NX, BLOCK, 128), f32),
            vmem((T, 2, NX, BLOCK, UNITS), f32),
            vmem((T, NX, BLOCK, 128), f32),
            vmem((T, 2, NX, BLOCK, UNITS), bf),
            vmem((K, 4, CHUNK, UNITS), bf),
            vmem((K, 2, UNITS, CHUNK), bf),
            vmem((T, K, 2, BLOCK // 2, CHUNK), bf),
            vmem((T, K, 2, BLOCK // 2, CHUNK), bf),
            vmem((T, K, 2, 2, BLOCK // 2, CHUNK), bf),
            vmem((T, K, 2, 2, BLOCK // 2, CHUNK), bf),
            vmem((T, K, NY, PACK, CHUNK), bf),
            vmem((T, K, NY, PACK, CHUNK), bf),
            vmem((T, K, 4, TOK, CHUNK), bf),
            vmem((8, 128), f32),
            vmem((4 * TOK, 128), f32),
            vmem((T, 4 * PACK, 4 * TOK), bf),
            vmem((T, 4 * TOK, 4 * PACK), bf),
            vmem((T, 4 * TOK, 128), f32),
            dma(K, 2), dma(K, 3), dma(2),
            dma(K, 2), dma(K, 2), dma(K, 3), dma(K, 3), dma(2), dma(2),
            dma(T, K, 3), dma(T, K, 3), dma(T, K, 2), dma(T, K, 2), dma(T, K, 2), dma(T, K, 2),
            dma(T, 3, NX), dma(T, 3, NX), dma(T, NX), dma(T, NX),
            dma(T, K, 2), dma(T, K, 2), dma(T, K, 2), dma(T, K, 2),
            dma(T, K, 3), dma(T, K, 3), dma(K, 2), dma(K, 2), dma(K, 2, 2), dma(K, 2, 2),
        ],
        compiler_params=pltpu.CompilerParams(
            collective_id=0, has_side_effects=True, vmem_limit_bytes=60 * 2**20),
    )(forward_in[0], reverse_in[0], gain, gate_up_weight[0], down_weight[0], table_row, table_col)
    return tuple(v[None] for v in outs)


def solution(mesh):
    in_specs = (
        P("section", "expert", None),
        P("section", "expert", None),
        P("section", None),
        P("section", None, None, "expert"),
        P("section", "expert", None),
        P("section", None, None, "expert", None),
        P("section", None, None, "expert", None),
    )
    out_specs = (P("section", "expert", None), P("section", "expert", None))
    return jax.shard_map(local, mesh=mesh, in_specs=in_specs, out_specs=out_specs, check_vma=False)
```

time: 453 us -> 160 us (0.35)
  waiting for transfers between devices: 295 us -> 0 us
  Pallas kernels: 0 us -> 150 us
  starting transfers between devices: 74.8 us -> 0 us
  local copies, waits for them, and re-layouts: 36.2 us -> 5.61 us
  matrix products: 27.2 us -> 0 us
  other arithmetic: 15.9 us -> 3.15 us
    all_to_all x8 -> x0, waiting for transfers between devices: 274 us -> none  [the longest x4 141 us: pass_layer(): lax.all_to_all(outgoing, 'expert', split_axis=0, concat_axis=0, tiled=True)]
    pallas_call x0 -> x1, Pallas kernels: none -> 150 us  [local(): pl.pallas_call(kernel, out_shape=(out, out), in_specs=[anywhere, anywhere...]
    all_to_all x8 -> x0, starting transfers between devices: 59.9 us -> none  [the longest x4 30.9 us: pass_layer(): lax.all_to_all(outgoing, 'expert', split_axis=0, concat_axis=0, tiled=True)]
    dot_general x16 -> x0, matrix products: 27.2 us -> none  [the longest x4 19.3 us: expert_share(): jnp.einsum('rd,kdu->kru', flat_rows, weight_in, preferred_element_type=jn...]
    reshape x16 -> x0, local copies, waits for them, and re-layouts: 24.8 us -> none  [the longest x4 12.9 us: expert_share(): flat_rows = received.reshape(sources * slots, width)]
    ppermute x4 -> x0, waiting for transfers between devices: 21.6 us -> none  [passed_along(): return lax.ppermute(block, axis, route)]
    ppermute x4 -> x0, starting transfers between devices: 14.9 us -> none  [passed_along(): return lax.ppermute(block, axis, route)]
    reduce_sum x10 -> x1, other arithmetic: 13.6 us -> 0.97 us  [local(): jnp.sum((ids[:, :, :, None] == ids[:, :, None, :]) & earlier, axis=-1)]
  transfers between devices with their start and end apart: 12 -> 0, of which waited for: 11 -> 0; matrix products, arithmetic and copies ran while one was open for 14% -> 0% of each run, Pallas kernels for 0% -> 0%
where the time goes in v1:
time: 160 us
  Pallas kernels  150 us (94%)
  local copies, waits for them, and re-layouts  5.61 us (4%)
  other arithmetic  3.15 us (2%)
    pallas_call x1, Pallas kernels, local(): pl.pallas_call(kernel, out_shape=(out, out), in_specs=[anywhere, anywhere...  150 us
    unnamed x2, local copies, waits for them, and re-layouts  3.28 us

profile of v1, /device:TPU:1, one launch (start us, length us, event | category | flops | bytes accessed | tf_op | source)
XLA Modules:
  0.0 159.7 jit_solution(5831099537376756412)
XLA Ops:
  0.6 0.1 broadcast_in_dim.51
  0.7 0.1 broadcast_in_dim.52
  0.8 1.0 convert_reduce_fusion
  1.8 0.8 add_convert_fusion
  2.6 0.1 broadcast_in_dim.55
  2.6 0.7 broadcast_in_dim.58
  3.3 0.1 broadcast_in_dim.59
  3.4 0.6 pad.8.mrow
  4.0 1.4 convert.1.gain
  5.4 0.1 copy.13
  5.5 0.6 pad.9.mcol
  6.1 150.3 %shard_map.86 = (bf16[16,7168]{1,0:T(8,128)(2,1)}, bf16[16,7168]{1,0:T(8,128)(2,1)}) custom-call(bf16[16,7168]{1,0:T(8,128)(2,1)} %bitcast.15, bf16[16,7168]{1,0:T(8,128)(2,1)} %bitcast.16, f32[14,1,512]{2,1,0:T(1,128)} %convert.1.gain, bf16[2,7168,256]{2,1,0:T(8,128)(2,1)} %bitcast.11, bf16[256,7168]{1,0:T(8,128)(2,1)} %bitcast.12, f32[8,128]{1,0:T(8,128)} %pad.8.mrow, ...), custom_call_target="tpu_custom_call" | custom-call | tf_op jit(solution)/shard_map/pallas_call | solution.py:391
  156.4 1.6 %copy.16 = bf16[1,16,7168]{2,1,0:T(8,128)(2,1)} copy(bf16[1,16,7168]{2,1,0:T(8,128)(2,1)} %bitcast.14) | data formatting | bytes 458752
  158.1 1.6 %copy.17 = bf16[1,16,7168]{2,1,0:T(8,128)(2,1)} copy(bf16[1,16,7168]{2,1,0:T(8,128)(2,1)} %bitcast.13) | data formatting | bytes 458752
  (6 shorter events, 0.0 us)

commit v2 on v1

v2 whole, which is shorter than its diff:
```python
import functools

import jax
import jax.numpy as jnp
from jax import lax
from jax.experimental import pallas as pl
from jax.experimental.pallas import tpu as pltpu
from jax.sharding import PartitionSpec as P

EXPERTS = 4
TICKS = 2
MOST = 6
WIDTH = 7168
HALF = WIDTH // 2
CHUNK = 512
SUB = CHUNK // 2
STEPS = HALF // CHUNK
NX = NY = 4
PACK = 4 * MOST
BLOCK = NY * PACK
UNITS = 256
TOK = 16
ROWS = 4 * TOK
MESH = pl.DeviceIdType.MESH
LAG_FIRST, LAG_BOTH, LAG_LAST = (0, 2, 4), (0, 2, 4, 6, 8, 10), (0, 2, 4, 6)


def kernel(
    fwd, rev, gain_in, wgu, wdn, table,
    outf, outr,
    rows, nb, pk, yb, xi, acc, ss, exg, exs, hid, wg, wd,
    cs, cr, yrs, yrr, zs, zo, zl, zr, ls, la, lb, tab, pick, pickt, mix, gain,
    sem_row, sem_w,
    t_s, t_r, row_s, row_r, w_s, w_r,
    yd_s, yd_r, xd_s, xd_r, ex_s, ex_r, hd_s, hd_r,
    cx_s, cx_r, yr_s, yr_r, z_s, z_r, l_s, l_r,
):
    s = lax.axis_index("section")
    me = lax.axis_index("expert")
    ns = lax.axis_size("section")
    c = lax.rem(me, 2)
    o = 1 - c
    x = lax.rem(me // 2, NX)
    y = me // (2 * NX)
    xp, xm = lax.rem(x + 1, NX), lax.rem(x + NX - 1, NX)
    sz = (lax.rem(s + 1, ns), lax.rem(s + ns - 1, ns))
    f32, bf16 = jnp.float32, jnp.bfloat16

    def at(xx, cc, yy=y, zz=s):
        return (zz, (yy * NX + xx) * 2 + cc)

    partner = at(x, o)
    sides = (at(xp, c), at(xm, c))
    ups = [at(x, c, lax.rem(y + j, NY)) for j in range(1, NY)]

    def rcopy(src, dst, ssem, rsem, dev):
        return pltpu.make_async_remote_copy(
            src_ref=src, dst_ref=dst, send_sem=ssem, recv_sem=rsem, device_id=dev, device_id_type=MESH)

    def arrival(spot, ssem, rsem):
        return rcopy(spot, spot, ssem, rsem, partner)

    barrier = pltpu.get_barrier_semaphore()
    peers = [partner] + [at(xx, cc) for xx in (xp, xm) for cc in (c, o)] + ups
    peers += [at(xx, cc, y, zz) for zz in sz for xx in (x, xp, xm) for cc in (c, o)]
    for dev in peers:
        pl.semaphore_signal(barrier, inc=1, device_id=dev, device_id_type=MESH)
    pl.semaphore_wait(barrier, len(peers))

    def col(half, k):
        return pl.ds(pl.multiple_of(half * HALF + k * CHUNK, CHUNK), CHUNK)

    def sub(half, k, h):
        return pl.ds(pl.multiple_of(half * HALF + k * CHUNK + h * SUB, SUB), SUB)

    def table_sends():
        made = [rcopy(table, tab.at[0], t_s.at[0], t_r.at[0], partner)]
        for cc in range(2):
            made.append(rcopy(table, tab.at[1 + c], t_s.at[1 + cc], t_r.at[1 + c], at(xp, cc)))
            made.append(rcopy(table, tab.at[3 + c], t_s.at[3 + cc], t_r.at[3 + c], at(xm, cc)))
        return made

    def row_here(k, d):
        return pltpu.make_async_copy((fwd, rev)[d].at[:, col(c, k)], rows.at[0, k, 2 * d + c], sem_row.at[k, d])

    def row_sends(k, d):
        src = (fwd, rev)[d]
        made = [rcopy(src.at[:, col(o, k)], rows.at[0, k, 2 * d + c], row_s.at[k, d, 0], row_r.at[k, d, 0], partner)]
        for cc in range(2):
            made.append(rcopy(
                src.at[:, sub(cc, k, 0)], nb.at[0, k, 0, 2 * d + c], row_s.at[k, d, 1 + cc], row_r.at[k, d, 1 + c],
                at(xp, cc)))
            made.append(rcopy(
                src.at[:, sub(cc, k, 1)], nb.at[0, k, 1, 2 * d + c], row_s.at[k, d, 3 + cc], row_r.at[k, d, 3 + c],
                at(xm, cc)))
        return made

    def row_arrivals(k, d):
        made = [arrival(rows.at[0, k, 2 * d + o], row_s.at[k, d, 0], row_r.at[k, d, 0])]
        for h in range(2):
            for cc in range(2):
                made.append(arrival(
                    nb.at[0, k, h, 2 * d + cc], row_s.at[k, d, 1 + 2 * h + cc], row_r.at[k, d, 1 + 2 * h + cc]))
        return made

    def weights_here(k):
        made = [pltpu.make_async_copy(wgu.at[g, col(c, k), :], wg.at[k, 2 * g + c], sem_w.at[k, g]) for g in range(2)]
        return made + [pltpu.make_async_copy(wdn.at[:, col(c, k)], wd.at[k, c], sem_w.at[k, 2])]

    def weight_sends(k):
        made = [
            rcopy(wgu.at[g, col(o, k), :], wg.at[k, 2 * g + c], w_s.at[k, g], w_r.at[k, g], partner) for g in range(2)]
        return made + [rcopy(wdn.at[:, col(o, k)], wd.at[k, c], w_s.at[k, 2], w_r.at[k, 2], partner)]

    def weight_arrivals(k):
        made = [arrival(wg.at[k, 2 * g + o], w_s.at[k, g], w_r.at[k, g]) for g in range(2)]
        return made + [arrival(wd.at[k, o], w_s.at[k, 2], w_r.at[k, 2])]

    def start_weights(k):
        for cp in weights_here(k) + weight_sends(k):
            cp.start()

    for cp in table_sends():
        cp.start()

    @pl.loop(0, STEPS)
    def _(k):
        for d in range(2):
            for cp in [row_here(k, d)] + row_sends(k, d):
                cp.start()

    for i in range(2 * STEPS):
        gain[i] = gain_in[:, i * CHUNK:(i + 1) * CHUNK].astype(f32)
    for i in range(5):
        arrival(tab.at[i], t_s.at[i], t_r.at[i]).wait_recv()

    row_no = lax.broadcasted_iota(jnp.int32, (ROWS, ROWS), 0)
    col_no = lax.broadcasted_iota(jnp.int32, (ROWS, ROWS), 1)
    same = (row_no // TOK) == (col_no // TOK)
    base_row = (lax.broadcasted_iota(jnp.int32, (1, ROWS), 1) // TOK * MOST).astype(f32)
    base_col = (lax.broadcasted_iota(jnp.int32, (ROWS, 1), 0) // TOK * MOST).astype(f32)
    slot = lax.broadcasted_iota(jnp.int32, (BLOCK, ROWS), 0).astype(f32)
    slot_t = lax.broadcasted_iota(jnp.int32, (ROWS, BLOCK), 1).astype(f32)

    def upright(v):
        return jnp.sum(jnp.where(row_no == col_no, v, 0.0), axis=1, keepdims=True)

    for whose, full in enumerate((table[...] + tab[0], tab[1] + tab[2], tab[3] + tab[4])):
        for t in range(TICKS):
            ids, share = full[t:t + 1, :ROWS], full[TICKS + t:TICKS + t + 1, :ROWS]
            ids_col = upright(ids)
            equal = same & (ids == ids_col)
            rank_col = jnp.sum(jnp.where(equal & (col_no < row_no), 1.0, 0.0), axis=1, keepdims=True)
            rank_row = jnp.sum(jnp.where(equal & (row_no < col_no), 1.0, 0.0), axis=0, keepdims=True)
            pick[whose, t] = jnp.where(slot == ids * PACK + base_row + rank_row, 1.0, 0.0).astype(bf16)
            pickt[whose, t] = jnp.where(slot_t == ids_col * PACK + base_col + rank_col, 1.0, 0.0).astype(bf16)
            mix[whose, t] = jnp.broadcast_to(upright(share), (ROWS, 128))

    def yd(t, k, j):
        e = lax.rem(y + j, NY)
        return rcopy(pk.at[t, k, e], yb.at[t, k, y], yd_s.at[t, k, j - 1], yd_r.at[t, k, j - 1], ups[j - 1])

    def z_sends(k, d):
        spots = (zo.at[k, d], zl.at[k, d], zr.at[k, d])
        parts = (zs.at[k, d], zs.at[k, d, pl.ds(0, 2)], zs.at[k, d, pl.ds(2, 2)])
        return [
            rcopy(parts[i], spots[i], z_s.at[k, d, i], z_r.at[k, d, i], at((x, xp, xm)[i], c, y, sz[d]))
            for i in range(3)]

    def d0(t, k):
        if t == 0:
            for d in range(2):
                row_here(k, d).wait()
                for cp in row_arrivals(k, d):
                    cp.wait_recv()
            left, right = nb[0, k, 0].reshape(ROWS, SUB), nb[0, k, 1].reshape(ROWS, SUB)
        else:
            for d in range(2):
                for i, spot in enumerate((zo.at[k, d], zl.at[k, d], zr.at[k, d])):
                    arrival(spot, z_s.at[k, d, i], z_r.at[k, d, i]).wait_recv()

            def added(a, b):
                return (a.astype(f32) + b.astype(f32)).astype(bf16)

            rows[1, k, :, :, :SUB] = added(zo[k, :, 0], zr[k, :, 1]).reshape(4, TOK, SUB)
            rows[1, k, :, :, SUB:] = added(zo[k, :, 2], zl[k, :, 1]).reshape(4, TOK, SUB)
            left = added(zl[k, :, 0], zo[k, :, 3]).reshape(ROWS, SUB)
            right = added(zr[k, :, 0], zo[k, :, 1]).reshape(ROWS, SUB)

        def packed(whose, v):
            made = jnp.dot(pick[whose, t], v, preferred_element_type=f32)
            return made.reshape(NY, PACK, v.shape[1]).astype(bf16)

        own = packed(0, rows[t, k].reshape(ROWS, CHUNK))
        pk[t, k, :, 0, 0] = packed(1, left)
        pk[t, k, :, 0, 1] = own[:, :, SUB:]
        pk[t, k, :, 1, 0] = own[:, :, :SUB]
        pk[t, k, :, 1, 1] = packed(2, right)
        for j in range(1, NY):
            yd(t, k, j).start()
        yb[t, k, y] = pk[t, k, y]

    def xd(t, k, way):
        return rcopy(yb.at[t, k, :, way], xi.at[t, k, way], xd_s.at[t, k, way], xd_r.at[t, k, way], sides[way])

    def d1(t, k):
        for j in range(1, NY):
            arrival(yb.at[t, k, lax.rem(y + NY - j, NY)], yd_s.at[t, k, j - 1], yd_r.at[t, k, j - 1]).wait_recv()
        for way in range(2):
            xd(t, k, way).start()

    def d2(t, k):
        for way in range(2):
            xd(t, k, way).wait_recv()
        if t == 0:
            for cp in weights_here(k):
                cp.wait()
            for cp in weight_arrivals(k):
                cp.wait_recv()

        def block(ref, way, h):
            v = ref[t, k, :, way, h] if ref is yb else ref[t, k, way, :, h]
            return v.astype(f32).reshape(BLOCK, SUB)

        first = jnp.concatenate([block(yb, 1, 0), block(xi, 1, 0), block(xi, 0, 0), block(yb, 0, 0)], axis=0)
        second = jnp.concatenate([block(yb, 0, 1), block(yb, 1, 1), block(xi, 1, 1), block(xi, 0, 1)], axis=0)
        held = jnp.concatenate([first, second], axis=1)
        square = held * held
        part = square[:, :128]
        for i in range(1, CHUNK // 128):
            part = part + square[:, 128 * i:128 * (i + 1)]
        scaled = (held * gain[c * STEPS + k]).astype(bf16)

        @pl.when(k == 0)
        def _():
            ss[t] = part.reshape(NX, BLOCK, 128)
            for q in range(4):
                acc[t, q] = jnp.dot(scaled, wg[k, q], preferred_element_type=f32).reshape(NX, BLOCK, UNITS)

        @pl.when(k > 0)
        def _():
            ss[t] += part.reshape(NX, BLOCK, 128)
            for q in range(4):
                acc[t, q] += jnp.dot(scaled, wg[k, q], preferred_element_type=f32).reshape(NX, BLOCK, UNITS)

    def ex(t, j):
        return [
            rcopy(acc.at[t, o, j], exg.at[t, 0, j], ex_s.at[t, 0, j], ex_r.at[t, 0, j], partner),
            rcopy(acc.at[t, 2 + o, j], exg.at[t, 1, j], ex_s.at[t, 1, j], ex_r.at[t, 1, j], partner),
            rcopy(ss.at[t, j], exs.at[t, j], ex_s.at[t, 2, j], ex_r.at[t, 2, j], partner),
        ]

    def hd(t, j):
        return rcopy(hid.at[t, c, j], hid.at[t, c, j], hd_s.at[t, j], hd_r.at[t, j], partner)

    def middle(t):
        for j in range(NX):
            for cp in ex(t, j):
                cp.start()

        @pl.loop(0, NX)
        def _(j):
            for cp in ex(t, j):
                cp.wait_recv()
            total = jnp.sum(ss[t, j] + exs[t, j], axis=-1, keepdims=True)
            scale = lax.rsqrt(total * (1.0 / WIDTH) + 1e-06)
            gate = (acc[t, c, j] + exg[t, 0, j]) * scale
            up = (acc[t, 2 + c, j] + exg[t, 1, j]) * scale
            hid[t, c, j] = (gate / (1.0 + jnp.exp(-gate)) * up).astype(bf16)
            hd(t, j).start()

        for j in range(NX):
            arrival(hid.at[t, o, j], hd_s.at[t, j], hd_r.at[t, j]).wait_recv()

    def down(t, k, j, h):
        return jnp.dot(hid[t, 0, j], wd[k, 0, :, h * SUB:(h + 1) * SUB], preferred_element_type=f32) + jnp.dot(
            hid[t, 1, j], wd[k, 1, :, h * SUB:(h + 1) * SUB], preferred_element_type=f32)

    def cx(t, k, way):
        return rcopy(cs.at[t, k, way], cr.at[t, k, way], cx_s.at[t, k, way], cx_r.at[t, k, way], sides[way])

    def c0(t, k):
        for way in range(2):
            for h in range(2):
                cs[t, k, way, h] = down(t, k, 1 + way + h, h).astype(bf16)
            cx(t, k, way).start()

    def yr(t, k, j):
        to = lax.rem(y + j, NY)
        return rcopy(yrs.at[t, k, to], yrr.at[t, k, y], yr_s.at[t, k, j - 1], yr_r.at[t, k, j - 1], ups[j - 1])

    def c1(t, k):
        for way in range(2):
            cx(t, k, way).wait_recv()
        for p in range(2):
            for h in range(2):
                j = 0 if p == 0 else (3, 1)[h]
                total = down(t, k, j, h) + cr[t, k, p ^ h, h].astype(f32)
                yrs[t, k, :, p, h] = total.reshape(NY, PACK, SUB).astype(bf16)
        for j in range(1, NY):
            yr(t, k, j).start()
        yrr[t, k, y] = yrs[t, k, y]

    def last_sends(k, d):
        made = []
        for cc in range(2):
            spot = ls.at[k, d, cc]
            made.append(rcopy(
                spot.at[pl.ds(0, 2)], la.at[k, d, c], l_s.at[k, d, cc, 0], l_r.at[k, d, c, 0], at(x, cc, y, sz[d])))
            made.append(rcopy(
                spot.at[2], lb.at[k, d, c, 0], l_s.at[k, d, cc, 1], l_r.at[k, d, c, 1], at(xm, cc, y, sz[d])))
            made.append(rcopy(
                spot.at[3], lb.at[k, d, c, 1], l_s.at[k, d, cc, 2], l_r.at[k, d, c, 2], at(xp, cc, y, sz[d])))
        return made

    def c2(t, k):
        for j in range(1, NY):
            arrival(yrr.at[t, k, lax.rem(y + NY - j, NY)], yr_s.at[t, k, j - 1], yr_r.at[t, k, j - 1]).wait_recv()

        def mine(whose, p, h):
            back = yrr[t, k, :, p, h].astype(f32).reshape(BLOCK, SUB).astype(bf16)
            return mix[whose, t][:, :1] * jnp.dot(pickt[whose, t], back, preferred_element_type=f32)

        kept = rows[t, k].reshape(ROWS, CHUNK).astype(f32)
        own = [(kept[:, h * SUB:(h + 1) * SUB] + mine(0, 0, h)).astype(bf16) for h in range(2)]
        left, right = mine(1, 1, 0).astype(bf16), mine(2, 1, 1).astype(bf16)
        if t == 0:
            for i, v in enumerate((own[0], right, own[1], left)):
                zs[k, :, i] = v.reshape(2, 2, TOK, SUB)
        else:
            for i, v in enumerate((own[0], own[1], left, right)):
                ls[k, :, :, i] = v.reshape(2, 2, TOK, SUB)
        for d in range(2):
            for cp in z_sends(k, d) if t == 0 else last_sends(k, d):
                cp.start()

    def finish(k):
        for d, out in enumerate((outf, outr)):
            for half in range(2):
                arrival(la.at[k, d, half], l_s.at[k, d, half, 0], l_r.at[k, d, half, 0]).wait_recv()
                for h in range(2):
                    arrival(lb.at[k, d, half, h], l_s.at[k, d, half, 1 + h], l_r.at[k, d, half, 1 + h]).wait_recv()
                for h in range(2):
                    out[:, sub(half, k, h)] = (
                        la[k, d, half, h].astype(f32) + lb[k, d, half, h].astype(f32)).astype(bf16)

    def run(stages):
        @pl.loop(0, STEPS + max(lag for lag, _ in stages))
        def _(i):
            for lag, f in stages:
                k = i - lag

                @pl.when((k >= 0) & (k < STEPS))
                def _():
                    f(k)

    def bound(t, *fs):
        return [functools.partial(f, t) for f in fs]

    run([(0, start_weights)] + list(zip(LAG_FIRST, bound(0, d0, d1, d2))))
    middle(0)
    run(list(zip(LAG_BOTH, bound(0, c0, c1, c2) + bound(1, d0, d1, d2))))
    middle(1)
    run(list(zip(LAG_LAST, bound(1, c0, c1, c2) + [finish])))

    for cp in table_sends():
        cp.wait_send()

    @pl.loop(0, STEPS)
    def _(k):
        for d in range(2):
            for cp in row_sends(k, d) + z_sends(k, d) + last_sends(k, d):
                cp.wait_send()
        for cp in weight_sends(k):
            cp.wait_send()
        for t in range(TICKS):
            for j in range(1, NY):
                yd(t, k, j).wait_send()
                yr(t, k, j).wait_send()
            for way in range(2):
                xd(t, k, way).wait_send()
                cx(t, k, way).wait_send()

    @pl.loop(0, NX)
    def _(j):
        for t in range(TICKS):
            for cp in ex(t, j):
                cp.wait_send()
            hd(t, j).wait_send()


def local(forward_in, reverse_in, norm_gain, gate_up_weight, down_weight, expert_ids, gate_weights):
    core = lax.rem(lax.axis_index("expert"), 2)
    f32, bf = jnp.float32, jnp.bfloat16
    both = jnp.concatenate([expert_ids.astype(f32), gate_weights], axis=0).reshape(2 * TICKS, 2, 1, TOK)
    own = (jnp.arange(2) == core)[None, None, :, None]
    table = jnp.where(own, both, 0.0).reshape(2 * TICKS, ROWS)
    table = jnp.pad(table, ((0, 8 - 2 * TICKS), (0, 128 - ROWS)))

    vmem = pltpu.VMEM
    dma = lambda *shape: pltpu.SemaphoreType.DMA(shape)
    anywhere = pl.BlockSpec(memory_space=pl.ANY)
    here = pl.BlockSpec(memory_space=pltpu.VMEM)
    T, K = TICKS, STEPS
    out = jax.ShapeDtypeStruct((TOK, WIDTH), bf)
    outs = pl.pallas_call(
        kernel,
        out_shape=(out, out),
        in_specs=[anywhere, anywhere, here, anywhere, anywhere, here],
        out_specs=(here, here),
        scratch_shapes=[
            vmem((T, K, 4, TOK, CHUNK), bf),
            vmem((1, K, 2, 4, TOK, SUB), bf),
            vmem((T, K, NY, 2, 2, PACK, SUB), bf),
            vmem((T, K, NY, 2, 2, PACK, SUB), bf),
            vmem((T, K, 2, NY, 2, PACK, SUB), bf),
            vmem((T, 4, NX, BLOCK, UNITS), f32),
            vmem((T, NX, BLOCK, 128), f32),
            vmem((T, 2, NX, BLOCK, UNITS), f32),
            vmem((T, NX, BLOCK, 128), f32),
            vmem((T, 2, NX, BLOCK, UNITS), bf),
            vmem((K, 4, CHUNK, UNITS), bf),
            vmem((K, 2, UNITS, CHUNK), bf),
            vmem((T, K, 2, 2, BLOCK, SUB), bf),
            vmem((T, K, 2, 2, BLOCK, SUB), bf),
            vmem((T, K, NY, 2, 2, PACK, SUB), bf),
            vmem((T, K, NY, 2, 2, PACK, SUB), bf),
            vmem((K, 2, 4, 2, TOK, SUB), bf),
            vmem((K, 2, 4, 2, TOK, SUB), bf),
            vmem((K, 2, 2, 2, TOK, SUB), bf),
            vmem((K, 2, 2, 2, TOK, SUB), bf),
            vmem((K, 2, 2, 4, TOK, SUB), bf),
            vmem((K, 2, 2, 2, TOK, SUB), bf),
            vmem((K, 2, 2, 2, TOK, SUB), bf),
            vmem((5, 8, 128), f32),
            vmem((3, T, BLOCK, ROWS), bf),
            vmem((3, T, ROWS, BLOCK), bf),
            vmem((3, T, ROWS, 128), f32),
            vmem((2 * K, 1, CHUNK), f32),
            dma(K, 2), dma(K, 3),
            dma(5), dma(5), dma(K, 2, 5), dma(K, 2, 5), dma(K, 3), dma(K, 3),
            dma(T, K, 3), dma(T, K, 3), dma(T, K, 2), dma(T, K, 2),
            dma(T, 3, NX), dma(T, 3, NX), dma(T, NX), dma(T, NX),
            dma(T, K, 2), dma(T, K, 2), dma(T, K, 3), dma(T, K, 3),
            dma(K, 2, 3), dma(K, 2, 3), dma(K, 2, 2, 3), dma(K, 2, 2, 3),
        ],
        compiler_params=pltpu.CompilerParams(
            collective_id=0, has_side_effects=True, vmem_limit_bytes=60 * 2**20),
    )(forward_in[0], reverse_in[0], norm_gain, gate_up_weight[0], down_weight[0], table)
    return tuple(v[None] for v in outs)


def solution(mesh):
    in_specs = (
        P("section", "expert", None),
        P("section", "expert", None),
        P("section", None),
        P("section", None, None, "expert"),
        P("section", "expert", None),
        P("section", None, None, "expert", None),
        P("section", None, None, "expert", None),
    )
    out_specs = (P("section", "expert", None), P("section", "expert", None))
    return jax.shard_map(local, mesh=mesh, in_specs=in_specs, out_specs=out_specs, check_vma=False)
```

time: 160 us -> 135 us (0.84)
  Pallas kernels: 150 us -> 129 us
  other arithmetic: 3.15 us -> 1.39 us
    pallas_call x1, Pallas kernels: 150 us -> 129 us  [local(): pl.pallas_call(kernel, out_shape=(out, out), in_specs=[anywhere, anywhere...]
where the time goes in v2:
time: 135 us
  Pallas kernels  129 us (96%)
  local copies, waits for them, and re-layouts  4.14 us (3%)
  other arithmetic  1.39 us (1%)
    pallas_call x1, Pallas kernels, local(): pl.pallas_call(kernel, out_shape=(out, out), in_specs=[anywhere, anywhere...  129 us
    unnamed x2, local copies, waits for them, and re-layouts  3.28 us

profile of v2, /device:TPU:1, one launch (start us, length us, event | category | flops | bytes accessed | tf_op | source)
XLA Modules:
  0.0 134.9 jit_solution(16528528868115458434)
XLA Ops:
  0.6 0.1 broadcast_in_dim.35
  0.7 0.1 broadcast_in_dim.36
  0.8 0.7 convert_element_type.5
  1.5 0.7 pad_maximum_fusion
  2.2 0.1 broadcast_in_dim.40
  2.3 0.6 pad.4.table
  2.9 128.7 %shard_map.86 = (bf16[16,7168]{1,0:T(8,128)(2,1)}, bf16[16,7168]{1,0:T(8,128)(2,1)}) custom-call(bf16[16,7168]{1,0:T(8,128)(2,1)} %bitcast.11, bf16[16,7168]{1,0:T(8,128)(2,1)} %bitcast.12, bf16[1,7168]{1,0:T(2,128)(2,1)} %gain_in.1, bf16[2,7168,256]{2,1,0:T(8,128)(2,1)} %bitcast.7, bf16[256,7168]{1,0:T(8,128)(2,1)} %bitcast.8, f32[8,128]{1,0:T(8,128)} %pad.4.table), custom_call_target="tpu_custom_call" | custom-call | tf_op jit(solution)/shard_map/pallas_call | solution.py:406
  131.6 1.6 %copy.11 = bf16[1,16,7168]{2,1,0:T(8,128)(2,1)} copy(bf16[1,16,7168]{2,1,0:T(8,128)(2,1)} %bitcast.10) | data formatting | bytes 458752
  133.2 1.6 %copy.12 = bf16[1,16,7168]{2,1,0:T(8,128)(2,1)} copy(bf16[1,16,7168]{2,1,0:T(8,128)(2,1)} %bitcast.9) | data formatting | bytes 458752
  (3 shorter events, 0.0 us)

commit v3 on v2

v3 whole, which is shorter than its diff:
```python
import functools

import jax
import jax.numpy as jnp
from jax import lax
from jax.experimental import pallas as pl
from jax.experimental.pallas import tpu as pltpu
from jax.sharding import PartitionSpec as P

EXPERTS = 4
TICKS = 2
MOST = 6
WIDTH = 7168
HALF = WIDTH // 2
CHUNK = 512
SUB = CHUNK // 2
STEPS = HALF // CHUNK
NX = NY = 4
SLOTS = 2 * MOST
PACK = 2 * SLOTS
BLOCK = NY * SLOTS
PACKS = NY * PACK
UNITS = 256
TOK = 16
ROWS = 2 * TOK
MESH = pl.DeviceIdType.MESH
LAGS = ((9, 5, 2, 1, 3, 4, 3), (3, 4, 2, 1, 5, 9, 7))
BEHIND = 7
ORDER = (2, 3, 4, 8, 0, 1, 9, 5, 6, 7)


def kernel(
    fwd, rev, gain_in, wgu, wdn, ids_in, share_in,
    outf, outr,
    rows, nb, pk, yb, xi, acc, ss, exg, exs, hid, wg, wd,
    cs, cr, yrs, yrr, zs, zo, zl, zr, ls, la, lb, tab, pick, pickt, mix, gain, apart, join, table,
    sem_row, sem_w,
    t_s, t_r, row_s, row_r, w_s, w_r,
    yd_s, yd_r, xd_s, xd_r, ex_s, ex_r, hd_s, hd_r,
    cx_s, cx_r, yr_s, yr_r, z_s, z_r, l_s, l_r,
):
    s = lax.axis_index("section")
    me = lax.axis_index("expert")
    ns = lax.axis_size("section")
    c = lax.rem(me, 2)
    o = 1 - c
    x = lax.rem(me // 2, NX)
    y = me // (2 * NX)
    xp, xm = lax.rem(x + 1, NX), lax.rem(x + NX - 1, NX)
    sz = (lax.rem(s + 1, ns), lax.rem(s + ns - 1, ns))
    f32, bf16 = jnp.float32, jnp.bfloat16

    def at(xx, cc, yy=y, zz=s):
        return (zz, (yy * NX + xx) * 2 + cc)

    partner = at(x, o)
    sides = (at(xp, c), at(xm, c))
    ups = [at(x, c, lax.rem(y + j, NY)) for j in range(1, NY)]

    def rcopy(src, dst, ssem, rsem, dev):
        return pltpu.make_async_remote_copy(
            src_ref=src, dst_ref=dst, send_sem=ssem, recv_sem=rsem, device_id=dev, device_id_type=MESH)

    def arrival(spot, ssem, rsem):
        return rcopy(spot, spot, ssem, rsem, partner)

    barrier = pltpu.get_barrier_semaphore()
    peers = [partner] + [at(xx, cc) for xx in (xp, xm) for cc in (c, o)] + ups
    peers += [at(xx, cc, y, zz) for zz in sz for xx in (x, xp, xm) for cc in (c, o)]
    for dev in peers:
        pl.semaphore_signal(barrier, inc=1, device_id=dev, device_id_type=MESH)

    for i in range(2 * STEPS):
        gain[i] = gain_in[:, i * CHUNK:(i + 1) * CHUNK].astype(f32)

    def number(shape, axis):
        return lax.broadcasted_iota(jnp.int32, shape, axis).astype(f32)

    lanes = lax.broadcasted_iota(jnp.int32, (TOK, 128), 1)
    token = lax.broadcasted_iota(jnp.int32, (TOK, 128), 0)
    group = lanes // TOK
    placed = (lanes - group * TOK == token) & ((group == c) | (group == 2 + c))
    listed = [ids_in[i].astype(f32) for i in range(4)] + [share_in[i] for i in range(4)]
    table[...] = jnp.dot(
        jnp.concatenate(listed, axis=0), jnp.where(placed, 1.0, 0.0), precision=lax.Precision.HIGHEST,
        preferred_element_type=f32)

    whole = jnp.floor((number((NX * BLOCK, 1), 0) + 0.5) * (1.0 / SLOTS))
    place = number((NX * BLOCK, 1), 0) + SLOTS * whole
    for h in range(2):
        apart[h] = jnp.where(number((NX * BLOCK, NX * PACKS), 1) == place + h * SLOTS, 1.0, 0.0).astype(bf16)
    whole = jnp.floor((number((PACKS, 1), 0) + 0.5) * (1.0 / PACK))
    inside = number((PACKS, 1), 0) - PACK * whole
    place = SLOTS * whole + inside + jnp.where(inside < SLOTS, 0.0, BLOCK - SLOTS)
    join[...] = jnp.where(number((PACKS, PACKS), 1) == place, 1.0, 0.0).astype(bf16)

    pl.semaphore_wait(barrier, len(peers))

    def col(half, k):
        return pl.ds(pl.multiple_of(half * HALF + k * CHUNK, CHUNK), CHUNK)

    def sub(half, k, h):
        return pl.ds(pl.multiple_of(half * HALF + k * CHUNK + h * SUB, SUB), SUB)

    def table_sends():
        made = [rcopy(table, tab.at[0], t_s.at[0], t_r.at[0], partner)]
        for cc in range(2):
            made.append(rcopy(table, tab.at[1 + c], t_s.at[1 + cc], t_r.at[1 + c], at(xp, cc)))
            made.append(rcopy(table, tab.at[3 + c], t_s.at[3 + cc], t_r.at[3 + c], at(xm, cc)))
        return made

    def row_here(d, k):
        return pltpu.make_async_copy((fwd, rev)[d].at[:, col(c, k)], rows.at[d, 0, k, c], sem_row.at[d, k])

    def row_sends(d, k):
        src = (fwd, rev)[d]
        made = [rcopy(src.at[:, col(o, k)], rows.at[d, 0, k, c], row_s.at[d, k, 0], row_r.at[d, k, 0], partner)]
        for cc in range(2):
            made.append(rcopy(
                src.at[:, sub(cc, k, 0)], nb.at[d, k, 0, c], row_s.at[d, k, 1 + cc], row_r.at[d, k, 1 + c], at(xp, cc)))
            made.append(rcopy(
                src.at[:, sub(cc, k, 1)], nb.at[d, k, 1, c], row_s.at[d, k, 3 + cc], row_r.at[d, k, 3 + c], at(xm, cc)))
        return made

    def row_arrivals(d, k):
        made = [arrival(rows.at[d, 0, k, o], row_s.at[d, k, 0], row_r.at[d, k, 0])]
        for h in range(2):
            for cc in range(2):
                i = 1 + 2 * h + cc
                made.append(arrival(nb.at[d, k, h, cc], row_s.at[d, k, i], row_r.at[d, k, i]))
        return made

    def weights_here(k):
        made = [pltpu.make_async_copy(wgu.at[g, col(c, k), :], wg.at[k, 2 * g + c], sem_w.at[k, g]) for g in range(2)]
        return made + [pltpu.make_async_copy(wdn.at[:, col(c, k)], wd.at[k, c], sem_w.at[k, 2])]

    def weight_sends(k):
        made = [
            rcopy(wgu.at[g, col(o, k), :], wg.at[k, 2 * g + c], w_s.at[k, g], w_r.at[k, g], partner) for g in range(2)]
        return made + [rcopy(wdn.at[:, col(o, k)], wd.at[k, c], w_s.at[k, 2], w_r.at[k, 2], partner)]

    def weight_arrivals(k):
        made = [arrival(wg.at[k, 2 * g + o], w_s.at[k, g], w_r.at[k, g]) for g in range(2)]
        return made + [arrival(wd.at[k, o], w_s.at[k, 2], w_r.at[k, 2])]

    def start_weights(k):
        for cp in weights_here(k) + weight_sends(k):
            cp.start()

    for cp in table_sends():
        cp.start()
    for d in range(2):

        @pl.loop(0, STEPS)
        def _(k):
            for cp in [row_here(d, k)] + row_sends(d, k):
                cp.start()

    for i in range(5):
        arrival(tab.at[i], t_s.at[i], t_r.at[i]).wait_recv()

    twice = 2 * ROWS
    row_no = lax.broadcasted_iota(jnp.int32, (twice, twice), 0)
    col_no = lax.broadcasted_iota(jnp.int32, (twice, twice), 1)
    same = (row_no // TOK) == (col_no // TOK)
    lane = lax.broadcasted_iota(jnp.int32, (1, twice), 1)
    line = lax.broadcasted_iota(jnp.int32, (twice, 1), 0)
    slot, slot_t = number((PACKS, twice), 0), number((twice, PACKS), 1)

    def core_of(v):
        return jnp.where((v // TOK == 1) | (v // TOK == 3), float(MOST), 0.0)

    def upright(v):
        return jnp.sum(jnp.where(row_no == col_no, v, 0.0), axis=1, keepdims=True)

    def onehot(v):
        return jnp.where(v, 1.0, 0.0).astype(bf16)

    full = (table[...] + tab[0], tab[1] + tab[2], tab[3] + tab[4])
    for d in range(2):
        for t in range(TICKS):
            found = []
            for one in full:
                ids = one[2 * t + d:2 * t + d + 1, :twice]
                share = upright(one[4 + 2 * t + d:5 + 2 * t + d, :twice])
                ids_col = upright(ids)
                equal = same & (ids == ids_col)
                rank_col = jnp.sum(jnp.where(equal & (col_no < row_no), 1.0, 0.0), axis=1, keepdims=True)
                rank_row = jnp.sum(jnp.where(equal & (row_no < col_no), 1.0, 0.0), axis=0, keepdims=True)
                found.append((
                    ids * PACK + core_of(lane) + rank_row, ids_col * PACK + core_of(line) + rank_col, share))
            own, left, right = found
            pick[d, t, 0] = onehot(slot == jnp.where(lane < ROWS, left[0], own[0] + SLOTS))
            pick[d, t, 1] = onehot(slot == jnp.where(lane < ROWS, own[0], right[0] + SLOTS))
            pickt[d, t, 0] = onehot(slot_t == jnp.where(line < ROWS, own[1], own[1] + SLOTS))
            pickt[d, t, 1] = onehot(slot_t == jnp.where(line < ROWS, left[1], right[1] + SLOTS))
            mix[d, t, 0] = jnp.broadcast_to(own[2], (twice, 128))
            mix[d, t, 1] = jnp.broadcast_to(jnp.where(line < ROWS, left[2], right[2]), (twice, 128))

    def yd(d, t, k, j):
        e = lax.rem(y + j, NY)
        return rcopy(
            pk.at[d, t, k, e], yb.at[d, t, k, y], yd_s.at[d, t, k, j - 1], yd_r.at[d, t, k, j - 1], ups[j - 1])

    def z_sends(d, k):
        spots = (zo.at[d, k], zl.at[d, k], zr.at[d, k])
        parts = (zs.at[d, k], zs.at[d, k, pl.ds(0, 2)], zs.at[d, k, pl.ds(2, 2)])
        return [
            rcopy(parts[i], spots[i], z_s.at[d, k, i], z_r.at[d, k, i], at((x, xp, xm)[i], c, y, sz[d]))
            for i in range(3)]

    def d0(d, t, k):
        if t == 0:
            row_here(d, k).wait()
            for cp in row_arrivals(d, k):
                cp.wait_recv()
            left, right = nb[d, k, 0].reshape(ROWS, SUB), nb[d, k, 1].reshape(ROWS, SUB)
        else:
            for i, spot in enumerate((zo.at[d, k], zl.at[d, k], zr.at[d, k])):
                arrival(spot, z_s.at[d, k, i], z_r.at[d, k, i]).wait_recv()

            def added(a, b):
                return (a.astype(f32) + b.astype(f32)).astype(bf16)

            rows[d, 1, k, :, :, :SUB] = added(zo[d, k, 0], zr[d, k, 1])
            rows[d, 1, k, :, :, SUB:] = added(zo[d, k, 2], zl[d, k, 1])
            left = added(zl[d, k, 0], zo[d, k, 3]).reshape(ROWS, SUB)
            right = added(zr[d, k, 0], zo[d, k, 1]).reshape(ROWS, SUB)
        own = rows[d, t, k].reshape(ROWS, CHUNK)
        for way, pair in enumerate(((left, own[:, SUB:]), (own[:, :SUB], right))):
            made = jnp.dot(pick[d, t, way], jnp.concatenate(pair, axis=0), preferred_element_type=f32)
            pk[d, t, k, :, way] = made.reshape(NY, PACK, SUB).astype(bf16)
        for j in range(1, NY):
            yd(d, t, k, j).start()
        yb[d, t, k, y] = pk[d, t, k, y]

    def xd(d, t, k, way):
        return rcopy(
            yb.at[d, t, k, :, way], xi.at[d, t, k, way], xd_s.at[d, t, k, way], xd_r.at[d, t, k, way], sides[way])

    def d1(d, t, k):
        for j in range(1, NY):
            spot = yb.at[d, t, k, lax.rem(y + NY - j, NY)]
            arrival(spot, yd_s.at[d, t, k, j - 1], yd_r.at[d, t, k, j - 1]).wait_recv()
        for way in range(2):
            xd(d, t, k, way).start()

    def d2(d, t, k):
        for way in range(2):
            xd(d, t, k, way).wait_recv()
        if d == 0 and t == 0:
            for cp in weights_here(k):
                cp.wait()
            for cp in weight_arrivals(k):
                cp.wait_recv()

        def flat(v):
            return v.astype(f32).reshape(PACKS, SUB).astype(bf16)

        mine = [flat(yb[d, t, k, :, way]) for way in range(2)]
        theirs = [flat(xi[d, t, k, way]) for way in range(2)]
        first = jnp.concatenate([mine[1], theirs[1], theirs[0], mine[0]], axis=0)
        second = jnp.concatenate([mine[0], mine[1], theirs[1], theirs[0]], axis=0)
        held = jnp.concatenate([
            jnp.dot(apart[0], first, preferred_element_type=f32),
            jnp.dot(apart[1], second, preferred_element_type=f32)], axis=1)
        square = held * held
        part = square[:, :128]
        for i in range(1, CHUNK // 128):
            part = part + square[:, 128 * i:128 * (i + 1)]
        scaled = (held * gain[c * STEPS + k]).astype(bf16)

        @pl.when(k == 0)
        def _():
            ss[d, t] = part.reshape(NX, BLOCK, 128)
            for q in range(4):
                acc[d, t, q] = jnp.dot(scaled, wg[k, q], preferred_element_type=f32).reshape(NX, BLOCK, UNITS)

        @pl.when(k > 0)
        def _():
            ss[d, t] += part.reshape(NX, BLOCK, 128)
            for q in range(4):
                acc[d, t, q] += jnp.dot(scaled, wg[k, q], preferred_element_type=f32).reshape(NX, BLOCK, UNITS)

    def ex(d, t):
        return [
            rcopy(acc.at[d, t, o], exg.at[d, t, 0], ex_s.at[d, t, 0], ex_r.at[d, t, 0], partner),
            rcopy(acc.at[d, t, 2 + o], exg.at[d, t, 1], ex_s.at[d, t, 1], ex_r.at[d, t, 1], partner),
            rcopy(ss.at[d, t], exs.at[d, t], ex_s.at[d, t, 2], ex_r.at[d, t, 2], partner),
        ]

    def hd(d, t):
        return rcopy(hid.at[d, t, c], hid.at[d, t, c], hd_s.at[d, t], hd_r.at[d, t], partner)

    def m0(d, t, k):
        for cp in ex(d, t):
            cp.start()

    def m1(d, t, k):
        for cp in ex(d, t):
            cp.wait_recv()

        @pl.loop(0, NX)
        def _(j):
            total = jnp.sum(ss[d, t, j] + exs[d, t, j], axis=-1, keepdims=True)
            scale = lax.rsqrt(total * (1.0 / WIDTH) + 1e-06)
            gate = (acc[d, t, c, j] + exg[d, t, 0, j]) * scale
            up = (acc[d, t, 2 + c, j] + exg[d, t, 1, j]) * scale
            hid[d, t, c, j] = (gate / (1.0 + jnp.exp(-gate)) * up).astype(bf16)

        hd(d, t).start()

    def m2(d, t, k):
        arrival(hid.at[d, t, o], hd_s.at[d, t], hd_r.at[d, t]).wait_recv()

    def down(d, t, k, js, h):
        total = None
        for cc in range(2):
            units = jnp.concatenate([hid[d, t, cc, j] for j in js], axis=0)
            made = jnp.dot(units, wd[k, cc, :, h * SUB:(h + 1) * SUB], preferred_element_type=f32)
            total = made if total is None else total + made
        return [total[i * BLOCK:(i + 1) * BLOCK] for i in range(len(js))]

    def cx(d, t, k, way):
        return rcopy(
            cs.at[d, t, k, way], cr.at[d, t, k, way], cx_s.at[d, t, k, way], cx_r.at[d, t, k, way], sides[way])

    def c0(d, t, k):
        for h in range(2):
            for way, v in enumerate(down(d, t, k, (1 + h, 2 + h), h)):
                cs[d, t, k, way, h] = v.astype(bf16)
        for way in range(2):
            cx(d, t, k, way).start()

    def yr(d, t, k, j):
        to = lax.rem(y + j, NY)
        return rcopy(
            yrs.at[d, t, k, to], yrr.at[d, t, k, y], yr_s.at[d, t, k, j - 1], yr_r.at[d, t, k, j - 1], ups[j - 1])

    def c1(d, t, k):
        for way in range(2):
            cx(d, t, k, way).wait_recv()
        both = [[], []]
        for h in range(2):
            for p, v in enumerate(down(d, t, k, (0, (3, 1)[h]), h)):
                both[p].append((v + cr[d, t, k, p ^ h, h].astype(f32)).astype(bf16))
        for p in range(2):
            made = jnp.dot(join[...], jnp.concatenate(both[p], axis=0), preferred_element_type=f32)
            yrs[d, t, k, :, p] = made.reshape(NY, PACK, SUB).astype(bf16)
        for j in range(1, NY):
            yr(d, t, k, j).start()
        yrr[d, t, k, y] = yrs[d, t, k, y]

    def last_sends(d, k):
        made = []
        for cc in range(2):
            spot = ls.at[d, k, cc]
            made.append(rcopy(
                spot.at[pl.ds(0, 2)], la.at[d, k, c], l_s.at[d, k, cc, 0], l_r.at[d, k, c, 0], at(x, cc, y, sz[d])))
            made.append(rcopy(
                spot.at[2], lb.at[d, k, c, 0], l_s.at[d, k, cc, 1], l_r.at[d, k, c, 1], at(xm, cc, y, sz[d])))
            made.append(rcopy(
                spot.at[3], lb.at[d, k, c, 1], l_s.at[d, k, cc, 2], l_r.at[d, k, c, 2], at(xp, cc, y, sz[d])))
        return made

    def c2(d, t, k):
        for j in range(1, NY):
            spot = yrr.at[d, t, k, lax.rem(y + NY - j, NY)]
            arrival(spot, yr_s.at[d, t, k, j - 1], yr_r.at[d, t, k, j - 1]).wait_recv()
        parts = []
        for p in range(2):
            back = yrr[d, t, k, :, p].astype(f32).reshape(PACKS, SUB).astype(bf16)
            got = mix[d, t, p][:, :1] * jnp.dot(pickt[d, t, p], back, preferred_element_type=f32)
            parts.append([got[h * ROWS:(h + 1) * ROWS] for h in range(2)])
        kept = rows[d, t, k].reshape(ROWS, CHUNK).astype(f32)
        own = [(kept[:, h * SUB:(h + 1) * SUB] + parts[0][h]).astype(bf16) for h in range(2)]
        left, right = parts[1][0].astype(bf16), parts[1][1].astype(bf16)
        if t == 0:
            for i, v in enumerate((own[0], right, own[1], left)):
                zs[d, k, i] = v.reshape(2, TOK, SUB)
        else:
            for i, v in enumerate((own[0], own[1], left, right)):
                ls[d, k, :, i] = v.reshape(2, TOK, SUB)
        for cp in z_sends(d, k) if t == 0 else last_sends(d, k):
            cp.start()

    def finish(d, t, k):
        out = (outf, outr)[d]
        for half in range(2):
            arrival(la.at[d, k, half], l_s.at[d, k, half, 0], l_r.at[d, k, half, 0]).wait_recv()
            for h in range(2):
                arrival(lb.at[d, k, half, h], l_s.at[d, k, half, 1 + h], l_r.at[d, k, half, 1 + h]).wait_recv()
            for h in range(2):
                out[:, sub(half, k, h)] = (la[d, k, half, h].astype(f32) + lb[d, k, half, h].astype(f32)).astype(bf16)

    starts = {}
    begin = 0
    for t in range(TICKS):
        x_send, gate_up, swap, hidden, x_sum, mixing, after = LAGS[t]
        starts[t, 0], starts[t, 1], starts[t, 2] = begin, begin + x_send, begin + x_send + gate_up
        starts[t, 3] = starts[t, 2] + STEPS - 1
        starts[t, 4] = starts[t, 3] + swap
        starts[t, 5] = starts[t, 6] = starts[t, 4] + hidden
        starts[t, 7] = starts[t, 6] + x_sum
        starts[t, 8] = starts[t, 7] + mixing
        begin = starts[t, 8] + after
    starts[TICKS - 1, 9] = begin
    stages = ((d0, STEPS), (d1, STEPS), (d2, STEPS), (m0, 1), (m1, 1), (m2, 1), (c0, STEPS), (c1, STEPS), (c2, STEPS),
              (finish, STEPS))

    @pl.loop(0, begin + STEPS + BEHIND)
    def _(i):
        @pl.when(i < STEPS)
        def _():
            start_weights(i)

        for stage in ORDER:
            f, count = stages[stage]
            for t in reversed(range(TICKS)):
                for d in range(2):
                    if (t, stage) in starts:
                        k = i - starts[t, stage] - d * BEHIND

                        @pl.when((k >= 0) & (k < count))
                        def _():
                            f(d, t, k)

    for cp in table_sends():
        cp.wait_send()
    for d in range(2):

        @pl.loop(0, STEPS)
        def _(k):
            for cp in row_sends(d, k) + z_sends(d, k) + last_sends(d, k):
                cp.wait_send()
            for t in range(TICKS):
                for j in range(1, NY):
                    yd(d, t, k, j).wait_send()
                    yr(d, t, k, j).wait_send()
                for way in range(2):
                    xd(d, t, k, way).wait_send()
                    cx(d, t, k, way).wait_send()

        for t in range(TICKS):
            for cp in ex(d, t):
                cp.wait_send()
            hd(d, t).wait_send()

    @pl.loop(0, STEPS)
    def _(k):
        for cp in weight_sends(k):
            cp.wait_send()


def local(forward_in, reverse_in, norm_gain, gate_up_weight, down_weight, expert_ids, gate_weights):
    f32, bf = jnp.float32, jnp.bfloat16
    vmem = pltpu.VMEM
    dma = lambda *shape: pltpu.SemaphoreType.DMA(shape)
    anywhere = pl.BlockSpec(memory_space=pl.ANY)
    here = pl.BlockSpec(memory_space=pltpu.VMEM)
    S, T, K = 2, TICKS, STEPS
    out = jax.ShapeDtypeStruct((TOK, WIDTH), bf)
    outs = pl.pallas_call(
        kernel,
        out_shape=(out, out),
        in_specs=[anywhere, anywhere, here, anywhere, anywhere, here, here],
        out_specs=(here, here),
        scratch_shapes=[
            vmem((S, T, K, 2, TOK, CHUNK), bf),
            vmem((S, K, 2, 2, TOK, SUB), bf),
            vmem((S, T, K, NY, 2, PACK, SUB), bf),
            vmem((S, T, K, NY, 2, PACK, SUB), bf),
            vmem((S, T, K, 2, NY, PACK, SUB), bf),
            vmem((S, T, 4, NX, BLOCK, UNITS), f32),
            vmem((S, T, NX, BLOCK, 128), f32),
            vmem((S, T, 2, NX, BLOCK, UNITS), f32),
            vmem((S, T, NX, BLOCK, 128), f32),
            vmem((S, T, 2, NX, BLOCK, UNITS), bf),
            vmem((K, 4, CHUNK, UNITS), bf),
            vmem((K, 2, UNITS, CHUNK), bf),
            vmem((S, T, K, 2, 2, BLOCK, SUB), bf),
            vmem((S, T, K, 2, 2, BLOCK, SUB), bf),
            vmem((S, T, K, NY, 2, PACK, SUB), bf),
            vmem((S, T, K, NY, 2, PACK, SUB), bf),
            vmem((S, K, 4, 2, TOK, SUB), bf),
            vmem((S, K, 4, 2, TOK, SUB), bf),
            vmem((S, K, 2, 2, TOK, SUB), bf),
            vmem((S, K, 2, 2, TOK, SUB), bf),
            vmem((S, K, 2, 4, TOK, SUB), bf),
            vmem((S, K, 2, 2, TOK, SUB), bf),
            vmem((S, K, 2, 2, TOK, SUB), bf),
            vmem((5, 8, 128), f32),
            vmem((S, T, 2, PACKS, 2 * ROWS), bf),
            vmem((S, T, 2, 2 * ROWS, PACKS), bf),
            vmem((S, T, 2, 2 * ROWS, 128), f32),
            vmem((2 * K, 1, CHUNK), f32),
            vmem((2, NX * BLOCK, NX * PACKS), bf),
            vmem((PACKS, PACKS), bf),
            vmem((8, 128), f32),
            dma(S, K), dma(K, 3),
            dma(5), dma(5), dma(S, K, 5), dma(S, K, 5), dma(K, 3), dma(K, 3),
            dma(S, T, K, 3), dma(S, T, K, 3), dma(S, T, K, 2), dma(S, T, K, 2),
            dma(S, T, 3), dma(S, T, 3), dma(S, T), dma(S, T),
            dma(S, T, K, 2), dma(S, T, K, 2), dma(S, T, K, 3), dma(S, T, K, 3),
            dma(S, K, 3), dma(S, K, 3), dma(S, K, 2, 3), dma(S, K, 2, 3),
        ],
        compiler_params=pltpu.CompilerParams(
            collective_id=0, has_side_effects=True, vmem_limit_bytes=50 * 2**20),
    )(forward_in[0], reverse_in[0], norm_gain, gate_up_weight[0], down_weight[0],
      expert_ids.reshape(2 * TICKS, 1, TOK), gate_weights.reshape(2 * TICKS, 1, TOK))
    return tuple(v[None] for v in outs)


def solution(mesh):
    in_specs = (
        P("section", "expert", None),
        P("section", "expert", None),
        P("section", None),
        P("section", None, None, "expert"),
        P("section", "expert", None),
        P("section", None, None, "expert", None),
        P("section", None, None, "expert", None),
    )
    out_specs = (P("section", "expert", None), P("section", "expert", None))
    return jax.shard_map(local, mesh=mesh, in_specs=in_specs, out_specs=out_specs, check_vma=False)
```

time: 135 us -> 133 us (0.985); the launches traced: 135 us -> 130 us
  Pallas kernels: 129 us -> 124 us
  other arithmetic: 1.39 us -> 0 us
    pallas_call x1, Pallas kernels: 129 us -> 124 us  [local(): pl.pallas_call(kernel, out_shape=(out, out), in_specs=[anywhere, anywhere...]
    unnamed x2 -> x12, local copies, waits for them, and re-layouts: 3.28 us -> 5.36 us
where the time goes in v3:
time: 133 us; the launch traced here: 130 us
  Pallas kernels  124 us (93%)
  local copies, waits for them, and re-layouts  5.36 us (4%)
    pallas_call x1, Pallas kernels, local(): pl.pallas_call(kernel, out_shape=(out, out), in_specs=[anywhere, anywhere...  124 us
    unnamed x12, local copies, waits for them, and re-layouts  5.36 us

profile of v3, /device:TPU:1, one launch (start us, length us, event | category | flops | bytes accessed | tf_op | source)
XLA Modules:
  0.0 130.5 jit_solution(11340618571502277189)
XLA Ops:
  0.6 0.0 copy-start
  0.6 0.9 copy-done
  1.6 0.0 copy-start.1
  1.6 0.9 copy-done.1
  2.5 0.0 copy-start.2
  2.5 0.7 copy-done.2
  3.3 0.0 copy-start.3
  3.3 0.7 copy-done.3
  3.9 0.0 copy-start.4
  3.9 0.7 copy-done.4
  4.6 124.5 %shard_map.86 = (bf16[16,7168]{1,0:T(8,128)(2,1)S(1)}, bf16[16,7168]{1,0:T(8,128)(2,1)S(1)}) custom-call(bf16[16,7168]{1,0:T(8,128)(2,1)S(1)} %bitcast.14, bf16[16,7168]{1,0:T(8,128)(2,1)S(1)} %bitcast.15, bf16[1,7168]{1,0:T(2,128)(2,1)S(1)} %copy-done.2, bf16[2,7168,256]{2,1,0:T(8,128)(2,1)} %bitcast.18, bf16[256,7168]{1,0:T(8,128)(2,1)} %bitcast.19, ...), custom_call_target="tpu_custom_call" | custom-call | tf_op jit(solution)/shard_map/pallas_call | solution.py:463
  129.1 0.7 copy.13
  129.8 0.7 copy.14
Async XLA Ops:
  0.6 0.9 copy-start
  1.6 0.9 copy-start.1
  2.5 0.7 copy-start.2
  3.3 0.7 copy-start.3
  3.9 0.7 copy-start.4

commit v4 on v2

--- a/solution.py
+++ b/solution.py
@@ -22,14 +22,14 @@
 TOK = 16
 ROWS = 4 * TOK
 MESH = pl.DeviceIdType.MESH
-LAG_FIRST, LAG_BOTH, LAG_LAST = (0, 2, 4), (0, 2, 4, 6, 8, 10), (0, 2, 4, 6)
+LAG_FIRST, LAG_BOTH, LAG_LAST = (0, 3, 6), (0, 2, 4, 6, 8, 10), (0, 3, 6, 9)
 
 
 def kernel(
-    fwd, rev, gain_in, wgu, wdn, table,
+    fwd, rev, gain_in, wgu, wdn, ids_in, share_in,
     outf, outr,
     rows, nb, pk, yb, xi, acc, ss, exg, exs, hid, wg, wd,
-    cs, cr, yrs, yrr, zs, zo, zl, zr, ls, la, lb, tab, pick, pickt, mix, gain,
+    cs, cr, yrs, yrr, zs, zo, zl, zr, ls, la, lb, tab, pick, pickt, mix, gain, table,
     sem_row, sem_w,
     t_s, t_r, row_s, row_r, w_s, w_r,
     yd_s, yd_r, xd_s, xd_r, ex_s, ex_r, hd_s, hd_r,
@@ -65,6 +65,23 @@
     peers += [at(xx, cc, y, zz) for zz in sz for xx in (x, xp, xm) for cc in (c, o)]
     for dev in peers:
         pl.semaphore_signal(barrier, inc=1, device_id=dev, device_id_type=MESH)
+
+    for i in range(2 * STEPS):
+        gain[i] = gain_in[:, i * CHUNK:(i + 1) * CHUNK].astype(f32)
+
+    lanes = lax.broadcasted_iota(jnp.int32, (TOK, 128), 1)
+    token = lax.broadcasted_iota(jnp.int32, (TOK, 128), 0)
+    group = lanes // TOK
+    filled = None
+    for d in range(2):
+        listed = [ids_in[2 * t + d].astype(f32) for t in range(TICKS)] + [share_in[2 * t + d] for t in range(TICKS)]
+        placed = (lanes - group * TOK == token) & (group == 2 * d + c)
+        part = jnp.dot(
+            jnp.concatenate(listed + listed, axis=0), jnp.where(placed, 1.0, 0.0), precision=lax.Precision.HIGHEST,
+            preferred_element_type=f32)
+        filled = part if filled is None else filled + part
+    table[...] = filled
+
     pl.semaphore_wait(barrier, len(peers))
 
     def col(half, k):
@@ -129,8 +146,6 @@
             for cp in [row_here(k, d)] + row_sends(k, d):
                 cp.start()
 
-    for i in range(2 * STEPS):
-        gain[i] = gain_in[:, i * CHUNK:(i + 1) * CHUNK].astype(f32)
     for i in range(5):
         arrival(tab.at[i], t_s.at[i], t_r.at[i]).wait_recv()
 
@@ -254,12 +269,13 @@
         return rcopy(hid.at[t, c, j], hid.at[t, c, j], hd_s.at[t, j], hd_r.at[t, j], partner)
 
     def middle(t):
-        for j in range(NX):
+        for j in (1, 2, 3, 0):
             for cp in ex(t, j):
                 cp.start()
 
         @pl.loop(0, NX)
-        def _(j):
+        def _(i):
+            j = lax.rem(i + 1, NX)
             for cp in ex(t, j):
                 cp.wait_recv()
             total = jnp.sum(ss[t, j] + exs[t, j], axis=-1, keepdims=True)
@@ -269,7 +285,7 @@
             hid[t, c, j] = (gate / (1.0 + jnp.exp(-gate)) * up).astype(bf16)
             hd(t, j).start()
 
-        for j in range(NX):
+        for j in range(1, NX):
             arrival(hid.at[t, o, j], hd_s.at[t, j], hd_r.at[t, j]).wait_recv()
 
     def down(t, k, j, h):
@@ -290,6 +306,10 @@
         return rcopy(yrs.at[t, k, to], yrr.at[t, k, y], yr_s.at[t, k, j - 1], yr_r.at[t, k, j - 1], ups[j - 1])
 
     def c1(t, k):
+        @pl.when(k == 0)
+        def _():
+            arrival(hid.at[t, o, 0], hd_s.at[t, 0], hd_r.at[t, 0]).wait_recv()
+
         for way in range(2):
             cx(t, k, way).wait_recv()
         for p in range(2):
@@ -390,13 +410,7 @@
 
 
 def local(forward_in, reverse_in, norm_gain, gate_up_weight, down_weight, expert_ids, gate_weights):
-    core = lax.rem(lax.axis_index("expert"), 2)
     f32, bf = jnp.float32, jnp.bfloat16
-    both = jnp.concatenate([expert_ids.astype(f32), gate_weights], axis=0).reshape(2 * TICKS, 2, 1, TOK)
-    own = (jnp.arange(2) == core)[None, None, :, None]
-    table = jnp.where(own, both, 0.0).reshape(2 * TICKS, ROWS)
-    table = jnp.pad(table, ((0, 8 - 2 * TICKS), (0, 128 - ROWS)))
-
     vmem = pltpu.VMEM
     dma = lambda *shape: pltpu.SemaphoreType.DMA(shape)
     anywhere = pl.BlockSpec(memory_space=pl.ANY)
@@ -406,7 +420,7 @@
     outs = pl.pallas_call(
         kernel,
         out_shape=(out, out),
-        in_specs=[anywhere, anywhere, here, anywhere, anywhere, here],
+        in_specs=[anywhere, anywhere, here, anywhere, anywhere, here, here],
         out_specs=(here, here),
         scratch_shapes=[
             vmem((T, K, 4, TOK, CHUNK), bf),
@@ -437,6 +451,7 @@
             vmem((3, T, ROWS, BLOCK), bf),
             vmem((3, T, ROWS, 128), f32),
             vmem((2 * K, 1, CHUNK), f32),
+            vmem((8, 128), f32),
             dma(K, 2), dma(K, 3),
             dma(5), dma(5), dma(K, 2, 5), dma(K, 2, 5), dma(K, 3), dma(K, 3),
             dma(T, K, 3), dma(T, K, 3), dma(T, K, 2), dma(T, K, 2),
@@ -445,8 +460,9 @@
             dma(K, 2, 3), dma(K, 2, 3), dma(K, 2, 2, 3), dma(K, 2, 2, 3),
         ],
         compiler_params=pltpu.CompilerParams(
-            collective_id=0, has_side_effects=True, vmem_limit_bytes=60 * 2**20),
-    )(forward_in[0], reverse_in[0], norm_gain, gate_up_weight[0], down_weight[0], table)
+            collective_id=0, has_side_effects=True, vmem_limit_bytes=50 * 2**20),
+    )(forward_in[0], reverse_in[0], norm_gain, gate_up_weight[0], down_weight[0],
+      expert_ids.reshape(2 * TICKS, 1, TOK), gate_weights.reshape(2 * TICKS, 1, TOK))
     return tuple(v[None] for v in outs)
 
 

time: 135 us -> 131 us (0.970)
  Pallas kernels: 129 us -> 125 us
  other arithmetic: 1.39 us -> 0 us
    pallas_call x1, Pallas kernels: 129 us -> 125 us  [local(): pl.pallas_call(kernel, out_shape=(out, out), in_specs=[anywhere, anywhere...]
    unnamed x2 -> x12, local copies, waits for them, and re-layouts: 3.28 us -> 5.36 us
where the time goes in v4:
time: 131 us
  Pallas kernels  125 us (95%)
  local copies, waits for them, and re-layouts  5.36 us (4%)
    pallas_call x1, Pallas kernels, local(): pl.pallas_call(kernel, out_shape=(out, out), in_specs=[anywhere, anywhere...  125 us
    unnamed x12, local copies, waits for them, and re-layouts  5.36 us

profile of v4, /device:TPU:1, one launch (start us, length us, event | category | flops | bytes accessed | tf_op | source)
XLA Modules:
  0.0 131.1 jit_solution(646691715664089112)
XLA Ops:
  0.6 0.0 copy-start
  0.6 0.9 copy-done
  1.6 0.0 copy-start.1
  1.6 0.9 copy-done.1
  2.5 0.0 copy-start.2
  2.5 0.7 copy-done.2
  3.3 0.0 copy-start.3
  3.3 0.7 copy-done.3
  3.9 0.0 copy-start.4
  3.9 0.7 copy-done.4
  4.6 125.0 %shard_map.86 = (bf16[16,7168]{1,0:T(8,128)(2,1)S(1)}, bf16[16,7168]{1,0:T(8,128)(2,1)S(1)}) custom-call(bf16[16,7168]{1,0:T(8,128)(2,1)S(1)} %bitcast.14, bf16[16,7168]{1,0:T(8,128)(2,1)S(1)} %bitcast.15, bf16[1,7168]{1,0:T(2,128)(2,1)S(1)} %copy-done.2, bf16[2,7168,256]{2,1,0:T(8,128)(2,1)} %bitcast.18, bf16[256,7168]{1,0:T(8,128)(2,1)} %bitcast.19, ...), custom_call_target="tpu_custom_call" | custom-call | tf_op jit(solution)/shard_map/pallas_call | solution.py:420
  129.7 0.7 copy.13
  130.4 0.7 copy.14
Async XLA Ops:
  0.6 0.9 copy-start
  1.6 0.9 copy-start.1
  2.5 0.7 copy-start.2
  3.3 0.7 copy-start.3
  3.9 0.7 copy-start.4
